TPU v7x, 128 devices: a whole 4x4x4 slice. The times are simulated.
128 devices in a mesh: freq: 16 (over x, z_lo, core), src: 8 (over y, z_hi).
Axes of the slice: x: 4, y: 4, z: 4 (z_hi: 2, z_lo: 2; z = z_hi * 2 + z_lo), core: 2. Of those that a mesh axis runs over, the one named last changes fastest.
Arguments:
- focusing: bfloat16 [64, 1024, 2048], P('src', 'freq'), may hold values from -6 to 6
- direct: bfloat16 [64, 1024, 2048], P('src', 'freq'), may hold values from -6 to 6
- kernel: bfloat16 [2, 192, 2048, 1024], P(None, 'freq', 'src'), may hold values from -0.125 to 0.125
- onset_up: int32 [64, 2048], P('freq', 'src'), may hold values from 256 to 2048
- onset_back: int32 [64, 1024], P('src', 'freq'), may hold values from 256 to 2048
Outputs:
- upgoing: bfloat16 [64, 2048, 2048], P('freq', 'src')
- updated: bfloat16 [64, 1024, 2048], P('src', 'freq')
All inputs are finite; a program needn't handle non-finite values.
Results may differ from a plain program's by a relative error of at most 0.008.
Values may be sent and summed in bfloat16 or wider, within the bound.
No kernel may reach another device: no remote copies, remote signals or barrier semaphores. Data moves between devices by JAX's collectives and lax.ppermute only.
A program may use at most 128 MiB of HBM per device.

v0:
```python
import functools
import math

import jax
import jax.numpy as jnp
from jax import lax
from jax.experimental import pallas as pl
from jax.experimental.pallas import tpu as pltpu
from jax.sharding import PartitionSpec as P


NT = 2048
NF = 192
BIN0 = 16
NFREQ = 16
NY = 4
J = NF // NFREQ
ROWS = 2 * NF
BLOCK = 2 * J
POINTS = 8
UP_POINTS = 4
RECV = 64
R = NFREQ * RECV
SOURCES = 256
SCALE = 2.0 / NT
F32 = jnp.float32
BF16 = jnp.bfloat16


NT_DIMS = (((1,), (1,)), ((), ()))
TN_DIMS = (((0,), (0,)), ((), ()))

OWN, UP, DOWN, FAR, ACROSS, ACROSS_UP, ACROSS_DOWN, ACROSS_FAR = range(8)
RELATIVE = ((0, 0), (3, 0), (1, 0), (2, 0), (0, 1), (3, 1), (1, 1), (2, 1))
NEAR = (OWN, UP, DOWN, ACROSS)
REMOTE = (FAR, ACROSS_UP, ACROSS_DOWN, ACROSS_FAR)


VMEM_SPEC = pl.BlockSpec(memory_space=pltpu.VMEM)
SMEM_SPEC = pl.BlockSpec(memory_space=pltpu.SMEM)
HBM_SPEC = pl.BlockSpec(memory_space=pltpu.HBM)


def params(limit=24):
    return pltpu.CompilerParams(
        dimension_semantics=("arbitrary",), vmem_limit_bytes=limit << 20
    )


def cost(flops, bytes_accessed):
    return pl.CostEstimate(flops=flops, bytes_accessed=bytes_accessed, transcendentals=0)


def turn(phase):
    quarter = (phase + NT // 8) >> 9
    rest = (phase - (quarter << 9)).astype(F32) * (2.0 * math.pi / NT)
    square = rest * rest
    sine = rest * (
        1.0 + square * (-1.0 / 6 + square * (1.0 / 120 + square * (-1.0 / 5040 + square / 362880)))
    )
    cosine = 1.0 + square * (
        -0.5 + square * (1.0 / 24 + square * (-1.0 / 720 + square * (1.0 / 40320 - square / 3628800)))
    )
    odd = (quarter & 1) == 1
    first, second = jnp.where(odd, sine, cosine), jnp.where(odd, cosine, sine)
    behind = ((quarter + 1) & 2) == 2
    below = (quarter & 2) == 2
    return jnp.where(behind, -first, first), jnp.where(below, -second, second)


def write_table(table):
    lane = lax.broadcasted_iota(jnp.int32, (ROWS, 128), 1)
    row = lax.broadcasted_iota(jnp.int32, (ROWS, 128), 0)
    bin_index = BIN0 + (row >> 1)
    quarter = row & 1
    fine_cos, fine_sin = turn((lane * bin_index) & (NT - 1))
    coarse_cos, coarse_sin = turn(((lane * bin_index + 4 * quarter) & 15) << 7)
    for a in range(NT // 128):
        value = coarse_cos[:, a : a + 1] * fine_cos - coarse_sin[:, a : a + 1] * fine_sin
        table[:, a * 128 : (a + 1) * 128] = value.astype(BF16)


def spectrum_body(traces, table, out):
    @pl.when(pl.program_id(0) == 0)
    def _():
        write_table(table)

    out[...] = lax.dot_general(
        table[...], traces[...], NT_DIMS, preferred_element_type=F32
    ).astype(BF16)


def spectrum(traces):
    count = traces.shape[0]
    tile = 128
    return pl.pallas_call(
        spectrum_body,
        grid=(count // tile,),
        in_specs=[pl.BlockSpec((tile, NT), lambda i: (i, 0))],
        out_specs=[
            pl.BlockSpec((ROWS, NT), lambda i: (0, 0)),
            pl.BlockSpec((ROWS, tile), lambda i: (0, i)),
        ],
        out_shape=[
            jax.ShapeDtypeStruct((ROWS, NT), BF16),
            jax.ShapeDtypeStruct((ROWS, count), BF16),
        ],
        compiler_params=params(),
        cost_estimate=cost(2 * count * NT * ROWS, 4 << 20),
        name="spectrum",
    )(traces)


def swapped(value, sign):
    rows, lanes = value.shape
    tiles = value.reshape(rows // 8, 2, 4, lanes)
    return jnp.concatenate([-sign * tiles[:, 1:], sign * tiles[:, :1]], axis=1).reshape(rows, lanes)


def places(me):
    y, z = me // 2, me % 2
    return [2 * ((y + dy) % NY) + (z + dz) % 2 for dy, dz in RELATIVE]


def hold_body(kern, held, sems):
    copies = [
        pltpu.make_async_copy(kern.at[part], held.at[part], sems.at[part]) for part in range(2)
    ]
    for copy in copies:
        copy.start()
    for copy in copies:
        copy.wait()


def hold(kern):
    return pl.pallas_call(
        hold_body,
        in_specs=[HBM_SPEC],
        out_specs=pl.BlockSpec(memory_space=pl.ANY),
        out_shape=pltpu.VMEM(kern.shape, BF16),
        scratch_shapes=[pltpu.SemaphoreType.DMA((2,))],
        compiler_params=pltpu.CompilerParams(vmem_limit_bytes=1 << 20),
        cost_estimate=cost(0, 13 << 20),
        name="hold",
    )(kern)


def waves_of(blocks, kern, j):
    field = jnp.concatenate([b[j] for b in blocks], axis=0)
    by_real = lax.dot_general(field, kern[0, j], NT_DIMS, preferred_element_type=F32)
    by_imag = lax.dot_general(field, kern[1, j], NT_DIMS, preferred_element_type=F32)
    waves = (by_real + swapped(by_imag, 1.0)).astype(BF16)
    return waves.reshape(len(blocks), 2, 8, SOURCES)


def forward_near_body(*refs):
    *blocks, kern, out = refs

    def step(j, carry):
        waves = waves_of(blocks, kern, j)
        for index in range(len(blocks)):
            for half in range(2):
                out[2 * index + half, j] = waves[index, half]
        return carry

    lax.fori_loop(0, J, step, 0)


def forward_near(blocks, kern):
    return pl.pallas_call(
        forward_near_body,
        in_specs=[VMEM_SPEC] * (len(blocks) + 1),
        out_specs=VMEM_SPEC,
        out_shape=jax.ShapeDtypeStruct((2 * len(blocks), J, 8, SOURCES), BF16),
        compiler_params=pltpu.CompilerParams(vmem_limit_bytes=8 << 20),
        cost_estimate=cost(4 * J * 64 * SOURCES * R, 2 << 20),
        name="forward_near",
    )(*blocks, kern)


def forward_body(me, near, *refs):
    *blocks, kern, out = refs
    place = places(me[0])
    for index, rel in enumerate(NEAR):
        for half in range(2):
            out[2 * place[rel] + half] = near[2 * index + half]

    def step(j, carry):
        waves = waves_of(blocks, kern, j)
        for index, rel in enumerate(REMOTE):
            for half in range(2):
                out[2 * place[rel] + half, j] = waves[index, half]
        return carry

    lax.fori_loop(0, J, step, 0)


def forward(me, near, blocks, kern):
    return pl.pallas_call(
        forward_body,
        in_specs=[SMEM_SPEC] + [VMEM_SPEC] * (len(blocks) + 2),
        out_specs=VMEM_SPEC,
        out_shape=jax.ShapeDtypeStruct((NFREQ, J, 8, SOURCES), BF16),
        compiler_params=pltpu.CompilerParams(vmem_limit_bytes=8 << 20),
        cost_estimate=cost(4 * J * 64 * SOURCES * R, 2 << 20),
        name="forward",
    )(me, near, *blocks, kern)


def terms_of(place, field_ref, held, which, outs, j):
    field = jnp.concatenate(
        [field_ref[2 * place[rel] + half, j] for rel in which for half in range(2)], axis=0
    )
    by_real = jnp.dot(field, held[0, j], preferred_element_type=F32)
    by_imag = jnp.dot(field, held[1, j], preferred_element_type=F32)
    terms = (by_real + swapped(by_imag, -1.0)).astype(BF16)
    for index in range(len(which)):
        outs[index][j] = terms[index * 16 : index * 16 + 16]


def adjoint_remote_body(me, field_ref, kern, *refs):
    *outs, held, sems = refs
    place = places(me[0])

    def copies(j):
        return [
            pltpu.make_async_copy(kern.at[part, j], held.at[part, j], sems.at[part, j])
            for part in range(2)
        ]

    for j in range(J):
        for copy in copies(j):
            copy.start()

    def step(j, carry):
        for copy in copies(j):
            copy.wait()
        terms_of(place, field_ref, held, REMOTE, outs, j)
        return carry

    lax.fori_loop(0, J, step, 0)


def adjoint_remote(me, field, kern):
    term = jax.ShapeDtypeStruct((J, 2 * POINTS, R), BF16)
    *terms, held = pl.pallas_call(
        adjoint_remote_body,
        in_specs=[SMEM_SPEC, VMEM_SPEC, HBM_SPEC],
        out_specs=[VMEM_SPEC] * (len(REMOTE) + 1),
        out_shape=[term] * len(REMOTE) + [pltpu.VMEM(kern.shape, BF16)],
        scratch_shapes=[pltpu.SemaphoreType.DMA((2, J))],
        compiler_params=pltpu.CompilerParams(vmem_limit_bytes=8 << 20),
        cost_estimate=cost(4 * J * 64 * SOURCES * R, 14 << 20),
        name="adjoint_remote",
    )(me, field, kern)
    return terms, held


def adjoint_near_body(me, field_ref, held, *outs):
    place = places(me[0])

    def step(j, carry):
        terms_of(place, field_ref, held, NEAR, outs, j)
        return carry

    lax.fori_loop(0, J, step, 0)


def adjoint_near(me, field, held):
    return pl.pallas_call(
        adjoint_near_body,
        in_specs=[SMEM_SPEC, VMEM_SPEC, VMEM_SPEC],
        out_specs=[VMEM_SPEC] * len(NEAR),
        out_shape=[jax.ShapeDtypeStruct((J, 2 * POINTS, R), BF16)] * len(NEAR),
        compiler_params=pltpu.CompilerParams(vmem_limit_bytes=8 << 20),
        cost_estimate=cost(4 * J * 64 * SOURCES * R, 2 << 20),
        name="adjoint_near",
    )(me, field, held)


def fold_body(*refs):
    *terms, out = refs
    low = lax.broadcasted_iota(jnp.int32, (8, 128), 1) < RECV

    def step(j, carry):
        total = functools.reduce(lambda a, b: a + b, [t[j].astype(F32) for t in terms])
        for pair in range(NFREQ // 2):
            first = total[:8, pair * 128 : pair * 128 + 128]
            second = total[8:, pair * 128 : pair * 128 + 128]
            out[2 * pair, j] = jnp.where(low, first, pltpu.roll(second, RECV, 1)).astype(BF16)
            out[2 * pair + 1, j] = jnp.where(low, pltpu.roll(first, RECV, 1), second).astype(BF16)
        return carry

    lax.fori_loop(0, J, step, 0)


def fold(terms):
    return pl.pallas_call(
        fold_body,
        in_specs=[VMEM_SPEC] * len(terms),
        out_specs=VMEM_SPEC,
        out_shape=jax.ShapeDtypeStruct((NFREQ, J, 8, 128), BF16),
        compiler_params=pltpu.CompilerParams(vmem_limit_bytes=8 << 20),
        cost_estimate=cost(0, 2 << 20),
        name="fold",
    )(*terms)


def truncate_body(waves, table, onset, up, back, wide_in, wide_out):
    step = pl.program_id(0)
    last = pl.num_programs(0) - 1

    @pl.when(step == 0)
    def _():
        for half in range(SOURCES // 128):
            wide_in[half] = waves[:, half * 128 : half * 128 + 128].astype(F32)

    every = pl.ds(step, ROWS, stride=UP_POINTS)
    mine = jnp.concatenate(
        [wide_in.at[half][every, :] for half in range(SOURCES // 128)], axis=1
    ).astype(BF16)
    signal = lax.dot_general(mine, table[...], TN_DIMS, preferred_element_type=F32) * SCALE
    sample = lax.broadcasted_iota(jnp.int32, signal.shape, 1)
    kept = jnp.where(sample < onset[...], signal, 0.0).astype(BF16)
    up[...] = kept
    bins = lax.dot_general(table[...], kept, NT_DIMS, preferred_element_type=F32)
    for half in range(SOURCES // 128):
        wide_out.at[half][every, :] = bins[:, half * 128 : half * 128 + 128]

    @pl.when(step == last)
    def _():
        for half in range(SOURCES // 128):
            back[:, half * 128 : half * 128 + 128] = wide_out[half].astype(BF16)


def truncate(waves, table, onset):
    rows = waves.shape[0]
    return pl.pallas_call(
        truncate_body,
        grid=(UP_POINTS,),
        in_specs=[
            pl.BlockSpec((rows, SOURCES), lambda i: (0, 0)),
            pl.BlockSpec((ROWS, NT), lambda i: (0, 0)),
            pl.BlockSpec((SOURCES, 1), lambda i: (i, 0)),
        ],
        out_specs=[
            pl.BlockSpec((SOURCES, NT), lambda i: (i, 0)),
            pl.BlockSpec((rows, SOURCES), lambda i: (0, 0)),
        ],
        out_shape=[
            jax.ShapeDtypeStruct((UP_POINTS * SOURCES, NT), BF16),
            jax.ShapeDtypeStruct((rows, SOURCES), BF16),
        ],
        scratch_shapes=[pltpu.VMEM((SOURCES // 128, rows, 128), F32)] * 2,
        compiler_params=params(),
        cost_estimate=cost(4 * UP_POINTS * SOURCES * NT * ROWS, 8 << 20),
        name="truncate",
    )(waves, table, onset)


def update_body(bins, table, direct, onset, out, wide):
    step = pl.program_id(0)

    @pl.when(step == 0)
    def _():
        wide[...] = bins[...].astype(F32)

    mine = wide[pl.ds(step, ROWS, stride=UP_POINTS), :].astype(BF16)
    trace = lax.dot_general(mine, table[...], TN_DIMS, preferred_element_type=F32) * SCALE
    sample = lax.broadcasted_iota(jnp.int32, trace.shape, 1)
    cut = jnp.where(sample < onset[...].reshape(2 * RECV, 1), trace, 0.0)
    value = (direct[...].reshape(2 * RECV, NT).astype(F32) - cut).astype(BF16)
    out[...] = value.reshape(out.shape)


def update(bins, table, direct, onset):
    rows = bins.shape[0]
    return pl.pallas_call(
        update_body,
        grid=(UP_POINTS,),
        in_specs=[
            pl.BlockSpec((rows, 2 * RECV), lambda i: (0, 0)),
            pl.BlockSpec((ROWS, NT), lambda i: (0, 0)),
            pl.BlockSpec((2, 1, RECV, NT), lambda i: (0, i, 0, 0)),
            pl.BlockSpec((2, 1, RECV, 1), lambda i: (0, i, 0, 0)),
        ],
        out_specs=pl.BlockSpec((2, 1, RECV, NT), lambda i: (0, i, 0, 0)),
        out_shape=jax.ShapeDtypeStruct((2, UP_POINTS, RECV, NT), BF16),
        scratch_shapes=[pltpu.VMEM((rows, 2 * RECV), F32)],
        compiler_params=params(),
        cost_estimate=cost(2 * POINTS * RECV * NT * ROWS, 6 << 20),
        name="update",
    )(bins, table, direct, onset)


def shift(value, dy, dz):
    pairs = [
        (2 * y + z, 2 * ((y + dy) % NY) + (z + dz) % 2) for y in range(NY) for z in range(2)
    ]
    return lax.ppermute(value, "src", pairs)


def add(*terms):
    return functools.reduce(lambda a, b: a + b, [t.astype(F32) for t in terms]).astype(BF16)


def exchange(value):
    return lax.all_to_all(value, "freq", split_axis=0, concat_axis=0, tiled=True)


def whole(focusing, direct, kernel, onset_up, onset_back):
    me = lax.axis_index("src").reshape(1)
    up_onset = onset_up.reshape(-1, 1)
    back_onset = onset_back.reshape(2, UP_POINTS, RECV, 1)
    kernel = pltpu.with_memory_space_constraint(kernel, pltpu.HBM)

    table, bins = spectrum(
        pltpu.with_memory_space_constraint(focusing.reshape(POINTS * RECV, NT), pltpu.HBM)
    )
    bins, me, up_onset, back_onset = lax.optimization_barrier((bins, me, up_onset, back_onset))
    bins = exchange(bins.reshape(NFREQ, BLOCK, POINTS * RECV))
    own = bins.reshape(NFREQ, J, 2, 2, UP_POINTS, RECV).transpose(1, 3, 2, 4, 0, 5)
    own = own.reshape(J, 2 * POINTS, R)
    own, late_kernel = lax.optimization_barrier((own, kernel))

    across = shift(own, 0, 1)
    up = shift(own, 1, 0)
    down = shift(own, -1, 0)
    held = hold(pltpu.with_memory_space_constraint(late_kernel, pltpu.HBM))
    across_down = shift(across, -1, 0)
    across_up = shift(across, 1, 0)
    far = shift(up, 1, 0)
    across_far = shift(across_down, -1, 0)
    near = forward_near([own, up, down, across], held)
    waves = exchange(forward(me, near, [far, across_up, across_down, across_far], held))

    upgoing, back = truncate(waves.reshape(NFREQ * J * 8, SOURCES), table, up_onset)
    back = exchange(back.reshape(NFREQ, J, 8, SOURCES))

    (far, across_up, across_down, across_far), held = adjoint_remote(me, back, kernel)
    own, up, down, across = adjoint_near(me, back, held)
    r1 = shift(across_far, 1, 0)
    r5 = shift(far, -1, 0)
    r3 = shift(across_up, -1, 0)
    r2 = shift(add(across_down, r1), 1, 0)
    r6 = shift(add(up, r5), -1, 0)
    r4 = shift(add(across, r2, r3), 0, 1)
    r7 = shift(down, 1, 0)
    summed = exchange(fold([own, r6, r7, r4]))

    updated = update(
        summed.reshape(NFREQ * J * 8, 2 * RECV),
        table,
        direct.reshape(2, UP_POINTS, RECV, NT),
        back_onset,
    )
    return (
        upgoing.reshape(UP_POINTS, SOURCES, NT),
        updated.reshape(POINTS, RECV, NT),
    )


def solution(mesh):
    placed = (
        P("src", "freq", None),
        P("src", "freq", None),
        P(None, "freq", "src", None),
        P("freq", "src"),
        P("src", "freq"),
    )
    return jax.shard_map(
        whole,
        mesh=mesh,
        in_specs=placed,
        out_specs=(P("freq", "src", None), P("src", "freq", None)),
        check_vma=False,
    )
```

profile of v0, /device:TPU:0, one launch (start us, length us, event | category | flops | bytes accessed | tf_op | source)
XLA Modules:
  0.0 172.2 jit_solution(9825412930717495301)
XLA Ops:
  0.6 6.0 %spectrum.1 = (bf16[384,2048]{1,0:T(8,128)(2,1)S(1)}, bf16[384,512]{1,0:T(8,128)(2,1)S(1)}) custom-call(bf16[512,2048]{1,0:T(8,128)(2,1)} %bitcast.27), custom_call_target="tpu_custom_call" | custom-call | flops 805306368 | bytes 4194304 | tf_op jit(solution)/shard_map/spectrum/pallas_call | solution.py:96
  7.4 14.7 %all_to_all.20 = bf16[16,24,512]{2,1,0:T(8,128)(2,1)S(1)} all-to-all(bf16[16,24,512]{2,1,0:T(8,128)(2,1)S(1)} %bitcast.21), channel_id=1, replica_groups=mesh['freq'=16,'src'=8] {'freq'}, dimensions={0} | all-to-all | bytes 786432 | tf_op jit(solution)/shard_map/all_to_all | solution.py:408
  24.0 3.7 %collective-permute-start.2 = (bf16[12,16,1024]{2,1,0:T(8,128)(2,1)S(1)}, bf16[12,16,1024]{2,1,0:T(8,128)(2,1)S(1)}, u32[]{:S(2)}, u32[]{:S(2)}) collective-permute-start(bf16[12,16,1024]{2,1,0:T(8,128)(2,1)S(1)} %reshape.49.refs_0_), channel_id=1, source_target_pairs={{0,1},{1,0},{2,3},{3,2},{4,5},{5,4},{6,7},{7,6},{8,9},{9,8},{10,11... | collective-permute-start | bytes 1179656 | tf_op jit(solution)/shard_map/ppermute | solution.py:400
  27.7 1.6 collective-permute-start
  29.3 7.6 %collective-permute-done.2.refs_3_ = bf16[12,16,1024]{2,1,0:T(8,128)(2,1)S(1)} collective-permute-done((bf16[12,16,1024]{2,1,0:T(8,128)(2,1)S(1)}, bf16[12,16,1024]{2,1,0:T(8,128)(2,1)S(1)}, u32[]{:S(2)}, u32[]{:S(2)}) %collective-permute-start.2) | collective-permute-done | bytes 393248 | tf_op jit(solution)/shard_map/ppermute | solution.py:400
  36.9 3.0 %collective-permute-start.5 = (bf16[12,16,1024]{2,1,0:T(8,128)(2,1)S(1)}, bf16[12,16,1024]{2,1,0:T(8,128)(2,1)S(1)}, u32[]{:S(2)}, u32[]{:S(2)}) collective-permute-start(bf16[12,16,1024]{2,1,0:T(8,128)(2,1)S(1)} %collective-permute-done.2.refs_3_), channel_id=1, source_target_pairs={{0,6},{1,7},{2,0},{3,1},{4,2},{5,3},{6,4},{7,5},{8,14},{9,15},{10,... | collective-permute-start | bytes 1179656 | tf_op jit(solution)/shard_map/ppermute | solution.py:400
  40.6 1.3 collective-permute-start.4
  42.0 7.5 %collective-permute-done.5.refs_2_ = bf16[12,16,1024]{2,1,0:T(8,128)(2,1)S(1)} collective-permute-done((bf16[12,16,1024]{2,1,0:T(8,128)(2,1)S(1)}, bf16[12,16,1024]{2,1,0:T(8,128)(2,1)S(1)}, u32[]{:S(2)}, u32[]{:S(2)}) %collective-permute-start.5) | collective-permute-done | bytes 393248 | tf_op jit(solution)/shard_map/ppermute | solution.py:400
  49.4 3.7 %collective-permute-start.6 = (bf16[12,16,1024]{2,1,0:T(8,128)(2,1)S(1)}, bf16[12,16,1024]{2,1,0:T(8,128)(2,1)S(1)}, u32[]{:S(2)}, u32[]{:S(2)}) collective-permute-start(bf16[12,16,1024]{2,1,0:T(8,128)(2,1)S(1)} %collective-permute-done.5.refs_2_), channel_id=1, source_target_pairs={{0,6},{1,7},{2,0},{3,1},{4,2},{5,3},{6,4},{7,5},{8,14},{9,15},{10,... | collective-permute-start | bytes 1179656 | tf_op jit(solution)/shard_map/ppermute | solution.py:400
  53.1 4.6 %hold.1.refs_4_ = bf16[2,12,256,1024]{3,2,1,0:T(8,128)(2,1)S(1)} custom-call(bf16[2,12,256,1024]{3,2,1,0:T(8,128)(2,1)} %kern.2), custom_call_target="tpu_custom_call" | custom-call | bytes 13631488 | tf_op jit(solution)/shard_map/hold/pallas_call | solution.py:136
  57.8 5.4 %forward_near.1.near = bf16[8,12,8,256]{3,2,1,0:T(8,128)(2,1)S(1)} custom-call(bf16[12,16,1024]{2,1,0:T(8,128)(2,1)S(1)} %reshape.49.refs_0_, bf16[12,16,1024]{2,1,0:T(8,128)(2,1)S(1)} %collective-permute-done.refs_1_, bf16[12,16,1024]{2,1,0:T(8,128)(2,1)S(1)} %collective-permute-done.1.refs_2_, bf16[12,16,1024]{2,1,0:T(8,128)(2,1)S(1)} %collective-permute-done.2.refs_3_, ...), custom_call_target="tpu_custom_call" | custom-call | flops 805306368 | bytes 2097152 | tf_op jit(solution)/shard_map/forward_near/pallas_call | solution.py:170
  63.2 1.4 collective-permute-done.6.refs_3_
  64.6 6.3 %forward.1 = bf16[16,12,8,256]{3,2,1,0:T(8,128)(2,1)} custom-call(s32[1]{0:T(128)} %bitcast.1.me, bf16[8,12,8,256]{3,2,1,0:T(8,128)(2,1)S(1)} %forward_near.1.near, bf16[12,16,1024]{2,1,0:T(8,128)(2,1)S(1)} %collective-permute-done.3.refs_0_, bf16[12,16,1024]{2,1,0:T(8,128)(2,1)S(1)} %collective-permute-done.4.refs_1_, ...), custom_call_target="tpu_custom_call" | custom-call | flops 805306368 | bytes 2097152 | tf_op jit(solution)/shard_map/forward/pallas_call | solution.py:199
  70.9 3.6 %all-to-all-start.1 = ((bf16[16,12,8,256]{3,2,1,0:T(8,128)(2,1)}), bf16[16,12,8,256]{3,2,1,0:T(8,128)(2,1)S(1)}, u32[]{:S(2)}, u32[]{:S(2)}) async-start(bf16[16,12,8,256]{3,2,1,0:T(8,128)(2,1)} %forward.1), calls=%async_computation.1 | async-start | bytes 1572864 | tf_op jit(solution)/shard_map/all_to_all | solution.py:408
  74.8 13.4 %all-to-all-done.1 = bf16[16,12,8,256]{3,2,1,0:T(8,128)(2,1)S(1)} async-done(((bf16[16,12,8,256]{3,2,1,0:T(8,128)(2,1)}), bf16[16,12,8,256]{3,2,1,0:T(8,128)(2,1)S(1)}, u32[]{:S(2)}, u32[]{:S(2)}) %all-to-all-start.1) | async-done | bytes 786464 | tf_op jit(solution)/shard_map/all_to_all | solution.py:408
  88.2 6.9 %truncate.1 = (bf16[1024,2048]{1,0:T(8,128)(2,1)}, bf16[1536,256]{1,0:T(8,128)(2,1)S(1)}) custom-call(bf16[1536,256]{1,0:T(8,128)(2,1)S(1)} %bitcast.19, bf16[384,2048]{1,0:T(8,128)(2,1)S(1)} %get-tuple-element.26.table, s32[1024,1]{1,0:T(8,128)S(1)} %copy.8.onset), custom_call_target="tpu_custom_call" | custom-call | flops 3221225472 | bytes 8388608 | tf_op jit(solution)/shard_map/truncate/pallas_call | solution.py:338
  95.0 15.9 %all_to_all.21.field_ref = bf16[16,12,8,256]{3,2,1,0:T(8,128)(2,1)S(1)} all-to-all(bf16[16,12,8,256]{3,2,1,0:T(8,128)(2,1)S(1)} %bitcast.20), channel_id=1, replica_groups=mesh['freq'=16,'src'=8] {'freq'}, dimensions={0} | all-to-all | bytes 1572864 | tf_op jit(solution)/shard_map/all_to_all | solution.py:408
  110.9 5.1 %adjoint_remote.1 = (bf16[12,16,1024]{2,1,0:T(8,128)(2,1)S(1)}, bf16[12,16,1024]{2,1,0:T(8,128)(2,1)S(1)}, bf16[12,16,1024]{2,1,0:T(8,128)(2,1)S(1)}, bf16[12,16...) custom-call(s32[1]{0:T(128)} %bitcast.1.me, bf16[16,12,8,256]{3,2,1,0:T(8,128)(2,1)S(1)} %all_to_all.21.field_ref, ...), custom_call_target="tpu_custom_call" | custom-call | flops 805306368 | bytes 14680064 | tf_op jit(solution)/shard_map/adjoint_remote/pallas_call | solution.py:246
  117.2 2.7 %collective-permute-start.7 = (bf16[12,16,1024]{2,1,0:T(8,128)(2,1)S(1)}, bf16[12,16,1024]{2,1,0:T(8,128)(2,1)S(1)}, u32[]{:S(2)}, u32[]{:S(2)}) collective-permute-start(bf16[12,16,1024]{2,1,0:T(8,128)(2,1)S(1)} %get-tuple-element.33), channel_id=1, source_target_pairs={{0,6},{1,7},{2,0},{3,1},{4,2},{5,3},{6,4},{7,5},{8,14},{9,15},{10,... | collective-permute-start | bytes 1179656 | tf_op jit(solution)/shard_map/ppermute | solution.py:400
  119.9 1.9 %collective-permute-start.12 = (bf16[12,16,1024]{2,1,0:T(8,128)(2,1)S(1)}, bf16[12,16,1024]{2,1,0:T(8,128)(2,1)S(1)}, u32[]{:S(2)}, u32[]{:S(2)}) collective-permute-start(bf16[12,16,1024]{2,1,0:T(8,128)(2,1)S(1)} %get-tuple-element.38), channel_id=1, source_target_pairs={{0,6},{1,7},{2,0},{3,1},{4,2},{5,3},{6,4},{7,5},{8,14},{9,15},{10,... | collective-permute-start | bytes 1179656 | tf_op jit(solution)/shard_map/ppermute | solution.py:400
  121.8 7.3 %collective-permute-done.10 = bf16[12,16,1024]{2,1,0:T(8,128)(2,1)S(1)} collective-permute-done((bf16[12,16,1024]{2,1,0:T(8,128)(2,1)S(1)}, bf16[12,16,1024]{2,1,0:T(8,128)(2,1)S(1)}, u32[]{:S(2)}, u32[]{:S(2)}) %collective-permute-start.10) | collective-permute-done | bytes 393248 | tf_op jit(solution)/shard_map/ppermute | solution.py:400
  129.6 3.6 %adjoint_near.1 = (bf16[12,16,1024]{2,1,0:T(8,128)(2,1)S(1)}, bf16[12,16,1024]{2,1,0:T(8,128)(2,1)S(1)}, bf16[12,16,1024]{2,1,0:T(8,128)(2,1)S(1)}, bf16[12,16,1024]{2,1,0:T(8,128)(2,1)S(1)}) custom-call(s32[1]{0:T(128)} %bitcast.1.me, bf16[16,12,8,256]{3,2,1,0:T(8,128)(2,1)S(1)} %all_to_all.21.field_ref, bf16[2,12,256,1024]{3,2,1,0:T(8,128)(2,1)S(1)} %get-tuple-element.30.held), custom_call_target="tpu_custom_call" | custom-call | flops 805306368 | bytes 2097152 | tf_op jit(solution)/shard_map/adjoint_near/pallas_call | solution.py:270
  134.1 2.7 %collective-permute-start.8 = (bf16[12,16,1024]{2,1,0:T(8,128)(2,1)S(1)}, bf16[12,16,1024]{2,1,0:T(8,128)(2,1)S(1)}, u32[]{:S(2)}, u32[]{:S(2)}) collective-permute-start(bf16[12,16,1024]{2,1,0:T(8,128)(2,1)S(1)} %add_convert_fusion.2), channel_id=1, source_target_pairs={{0,6},{1,7},{2,0},{3,1},{4,2},{5,3},{6,4},{7,5},{8,14},{9,15},{10,... | collective-permute-start | bytes 1179656 | tf_op jit(solution)/shard_map/ppermute | solution.py:400
  137.8 5.0 %collective-permute-done.11 = bf16[12,16,1024]{2,1,0:T(8,128)(2,1)S(1)} collective-permute-done((bf16[12,16,1024]{2,1,0:T(8,128)(2,1)S(1)}, bf16[12,16,1024]{2,1,0:T(8,128)(2,1)S(1)}, u32[]{:S(2)}, u32[]{:S(2)}) %collective-permute-start.11) | collective-permute-done | bytes 393248 | tf_op jit(solution)/shard_map/ppermute | solution.py:400
  142.9 3.0 %collective-permute-start.13 = (bf16[12,16,1024]{2,1,0:T(8,128)(2,1)S(1)}, bf16[12,16,1024]{2,1,0:T(8,128)(2,1)S(1)}, u32[]{:S(2)}, u32[]{:S(2)}) collective-permute-start(bf16[12,16,1024]{2,1,0:T(8,128)(2,1)S(1)} %add_convert_fusion), channel_id=1, source_target_pairs={{0,1},{1,0},{2,3},{3,2},{4,5},{5,4},{6,7},{7,6},{8,9},{9,8},{10,11... | collective-permute-start | bytes 1179656 | tf_op jit(solution)/shard_map/ppermute | solution.py:400
  146.0 3.7 %collective-permute-done.9.refs_2_ = bf16[12,16,1024]{2,1,0:T(8,128)(2,1)S(1)} collective-permute-done((bf16[12,16,1024]{2,1,0:T(8,128)(2,1)S(1)}, bf16[12,16,1024]{2,1,0:T(8,128)(2,1)S(1)}, u32[]{:S(2)}, u32[]{:S(2)}) %collective-permute-start.9) | collective-permute-done | bytes 393248 | tf_op jit(solution)/shard_map/ppermute | solution.py:400
  149.7 3.0 %collective-permute-done.13.refs_3_ = bf16[12,16,1024]{2,1,0:T(8,128)(2,1)S(1)} collective-permute-done((bf16[12,16,1024]{2,1,0:T(8,128)(2,1)S(1)}, bf16[12,16,1024]{2,1,0:T(8,128)(2,1)S(1)}, u32[]{:S(2)}, u32[]{:S(2)}) %collective-permute-start.13) | collective-permute-done | bytes 393248 | tf_op jit(solution)/shard_map/ppermute | solution.py:400
  152.7 1.8 %fold.1 = bf16[16,12,8,128]{3,2,1,0:T(8,128)(2,1)} custom-call(bf16[12,16,1024]{2,1,0:T(8,128)(2,1)S(1)} %get-tuple-element.31.refs_0_, bf16[12,16,1024]{2,1,0:T(8,128)(2,1)S(1)} %collective-permute-done.8.refs_1_, bf16[12,16,1024]{2,1,0:T(8,128)(2,1)S(1)} %collective-permute-done.9.refs_2_, bf16[12,16,1024]{2,1,0:T(8,128)(2,1)S(1)} %collective-permute-done.13.refs_3_), custom_call_target="tpu_custom_call" | custom-call | bytes 2097152 | tf_op jit(solution)/shard_map/fold/pallas_call | solution.py:298
  154.6 3.7 %all-to-all-start.3 = ((bf16[16,12,8,128]{3,2,1,0:T(8,128)(2,1)}), bf16[16,12,8,128]{3,2,1,0:T(8,128)(2,1)S(1)}, u32[]{:S(2)}, u32[]{:S(2)}) async-start(bf16[16,12,8,128]{3,2,1,0:T(8,128)(2,1)} %fold.1), calls=%async_computation.3 | async-start | bytes 786432 | tf_op jit(solution)/shard_map/all_to_all | solution.py:408
  158.5 8.9 %all-to-all-done.3 = bf16[16,12,8,128]{3,2,1,0:T(8,128)(2,1)S(1)} async-done(((bf16[16,12,8,128]{3,2,1,0:T(8,128)(2,1)}), bf16[16,12,8,128]{3,2,1,0:T(8,128)(2,1)S(1)}, u32[]{:S(2)}, u32[]{:S(2)}) %all-to-all-start.3) | async-done | bytes 393248 | tf_op jit(solution)/shard_map/all_to_all | solution.py:408
  167.4 1.4 copy-done.2
  168.8 3.4 %update.1 = bf16[2,4,64,2048]{3,2,1,0:T(8,128)(2,1)} custom-call(bf16[1536,128]{1,0:T(8,128)(2,1)S(1)} %bitcast.18, bf16[384,2048]{1,0:T(8,128)(2,1)S(1)} %copy-done.2, bf16[2,4,64,2048]{3,2,1,0:T(8,128)(2,1)S(1)} %bitcast.17, s32[2,4,64,1]{3,2,1,0:T(8,128)S(1)} %copy.9.onset), custom_call_target="tpu_custom_call" | custom-call | flops 805306368 | bytes 6291456 | tf_op jit(solution)/shard_map/update/pallas_call | solution.py:378
  (28 shorter events, 7.4 us)
Async XLA Ops:
  6.7 81.5 %copy-start.1 = (bf16[384,2048]{1,0:T(8,128)(2,1)}, bf16[384,2048]{1,0:T(8,128)(2,1)S(1)}, u32[]{:S(2)}) copy-start(bf16[384,2048]{1,0:T(8,128)(2,1)S(1)} %get-tuple-element.26.table) | copy-start | bytes 4718596
  24.0 12.9 %collective-permute-start.2 = (bf16[12,16,1024]{2,1,0:T(8,128)(2,1)S(1)}, bf16[12,16,1024]{2,1,0:T(8,128)(2,1)S(1)}, u32[]{:S(2)}, u32[]{:S(2)}) collective-permute-start(bf16[12,16,1024]{2,1,0:T(8,128)(2,1)S(1)} %reshape.49.refs_0_), channel_id=1, source_target_pairs={{0,1},{1,0},{2,3},{3,2},{4,5},{5,4},{6,7},{7,6},{8,9},{9,8},{10,11... | collective-permute-start | bytes 1179656 | tf_op jit(solution)/shard_map/ppermute | solution.py:400
  27.7 14.3 %collective-permute-start = (bf16[12,16,1024]{2,1,0:T(8,128)(2,1)S(1)}, bf16[12,16,1024]{2,1,0:T(8,128)(2,1)S(1)}, u32[]{:S(2)}, u32[]{:S(2)}) collective-permute-start(bf16[12,16,1024]{2,1,0:T(8,128)(2,1)S(1)} %reshape.49.refs_0_), channel_id=1, source_target_pairs={{0,2},{1,3},{2,4},{3,5},{4,6},{5,7},{6,0},{7,1},{8,10},{9,11},{10,... | collective-permute-start | bytes 1179656 | tf_op jit(solution)/shard_map/ppermute | solution.py:400
  36.9 12.5 %collective-permute-start.5 = (bf16[12,16,1024]{2,1,0:T(8,128)(2,1)S(1)}, bf16[12,16,1024]{2,1,0:T(8,128)(2,1)S(1)}, u32[]{:S(2)}, u32[]{:S(2)}) collective-permute-start(bf16[12,16,1024]{2,1,0:T(8,128)(2,1)S(1)} %collective-permute-done.2.refs_3_), channel_id=1, source_target_pairs={{0,6},{1,7},{2,0},{3,1},{4,2},{5,3},{6,4},{7,5},{8,14},{9,15},{10,... | collective-permute-start | bytes 1179656 | tf_op jit(solution)/shard_map/ppermute | solution.py:400
  39.9 17.9 %collective-permute-start.1 = (bf16[12,16,1024]{2,1,0:T(8,128)(2,1)S(1)}, bf16[12,16,1024]{2,1,0:T(8,128)(2,1)S(1)}, u32[]{:S(2)}, u32[]{:S(2)}) collective-permute-start(bf16[12,16,1024]{2,1,0:T(8,128)(2,1)S(1)} %reshape.49.refs_0_), channel_id=1, source_target_pairs={{0,6},{1,7},{2,0},{3,1},{4,2},{5,3},{6,4},{7,5},{8,14},{9,15},{10,... | collective-permute-start | bytes 1179656 | tf_op jit(solution)/shard_map/ppermute | solution.py:400
  40.6 22.5 %collective-permute-start.4 = (bf16[12,16,1024]{2,1,0:T(8,128)(2,1)S(1)}, bf16[12,16,1024]{2,1,0:T(8,128)(2,1)S(1)}, u32[]{:S(2)}, u32[]{:S(2)}) collective-permute-start(bf16[12,16,1024]{2,1,0:T(8,128)(2,1)S(1)} %collective-permute-done.2.refs_3_), channel_id=1, source_target_pairs={{0,2},{1,3},{2,4},{3,5},{4,6},{5,7},{6,0},{7,1},{8,10},{9,11},{10,... | collective-permute-start | bytes 1179656 | tf_op jit(solution)/shard_map/ppermute | solution.py:400
  41.9 21.3 %collective-permute-start.3 = (bf16[12,16,1024]{2,1,0:T(8,128)(2,1)S(1)}, bf16[12,16,1024]{2,1,0:T(8,128)(2,1)S(1)}, u32[]{:S(2)}, u32[]{:S(2)}) collective-permute-start(bf16[12,16,1024]{2,1,0:T(8,128)(2,1)S(1)} %collective-permute-done.refs_1_), channel_id=1, source_target_pairs={{0,2},{1,3},{2,4},{3,5},{4,6},{5,7},{6,0},{7,1},{8,10},{9,11},{10,... | collective-permute-start | bytes 1179656 | tf_op jit(solution)/shard_map/ppermute | solution.py:400
  49.4 15.2 %collective-permute-start.6 = (bf16[12,16,1024]{2,1,0:T(8,128)(2,1)S(1)}, bf16[12,16,1024]{2,1,0:T(8,128)(2,1)S(1)}, u32[]{:S(2)}, u32[]{:S(2)}) collective-permute-start(bf16[12,16,1024]{2,1,0:T(8,128)(2,1)S(1)} %collective-permute-done.5.refs_2_), channel_id=1, source_target_pairs={{0,6},{1,7},{2,0},{3,1},{4,2},{5,3},{6,4},{7,5},{8,14},{9,15},{10,... | collective-permute-start | bytes 1179656 | tf_op jit(solution)/shard_map/ppermute | solution.py:400
  70.9 17.2 %all-to-all-start.1 = ((bf16[16,12,8,256]{3,2,1,0:T(8,128)(2,1)}), bf16[16,12,8,256]{3,2,1,0:T(8,128)(2,1)S(1)}, u32[]{:S(2)}, u32[]{:S(2)}) async-start(bf16[16,12,8,256]{3,2,1,0:T(8,128)(2,1)} %forward.1), calls=%async_computation.1 | async-start | bytes 1572864 | tf_op jit(solution)/shard_map/all_to_all | solution.py:408
  116.0 13.1 %collective-permute-start.10 = (bf16[12,16,1024]{2,1,0:T(8,128)(2,1)S(1)}, bf16[12,16,1024]{2,1,0:T(8,128)(2,1)S(1)}, u32[]{:S(2)}, u32[]{:S(2)}) collective-permute-start(bf16[12,16,1024]{2,1,0:T(8,128)(2,1)S(1)} %get-tuple-element.37), channel_id=1, source_target_pairs={{0,2},{1,3},{2,4},{3,5},{4,6},{5,7},{6,0},{7,1},{8,10},{9,11},{10,... | collective-permute-start | bytes 1179656 | tf_op jit(solution)/shard_map/ppermute | solution.py:400
  117.2 16.8 %collective-permute-start.7 = (bf16[12,16,1024]{2,1,0:T(8,128)(2,1)S(1)}, bf16[12,16,1024]{2,1,0:T(8,128)(2,1)S(1)}, u32[]{:S(2)}, u32[]{:S(2)}) collective-permute-start(bf16[12,16,1024]{2,1,0:T(8,128)(2,1)S(1)} %get-tuple-element.33), channel_id=1, source_target_pairs={{0,6},{1,7},{2,0},{3,1},{4,2},{5,3},{6,4},{7,5},{8,14},{9,15},{10,... | collective-permute-start | bytes 1179656 | tf_op jit(solution)/shard_map/ppermute | solution.py:400
  119.9 17.9 %collective-permute-start.12 = (bf16[12,16,1024]{2,1,0:T(8,128)(2,1)S(1)}, bf16[12,16,1024]{2,1,0:T(8,128)(2,1)S(1)}, u32[]{:S(2)}, u32[]{:S(2)}) collective-permute-start(bf16[12,16,1024]{2,1,0:T(8,128)(2,1)S(1)} %get-tuple-element.38), channel_id=1, source_target_pairs={{0,6},{1,7},{2,0},{3,1},{4,2},{5,3},{6,4},{7,5},{8,14},{9,15},{10,... | collective-permute-start | bytes 1179656 | tf_op jit(solution)/shard_map/ppermute | solution.py:400
  129.3 13.4 %collective-permute-start.11 = (bf16[12,16,1024]{2,1,0:T(8,128)(2,1)S(1)}, bf16[12,16,1024]{2,1,0:T(8,128)(2,1)S(1)}, u32[]{:S(2)}, u32[]{:S(2)}) collective-permute-start(bf16[12,16,1024]{2,1,0:T(8,128)(2,1)S(1)} %add_convert_fusion.1), channel_id=1, source_target_pairs={{0,2},{1,3},{2,4},{3,5},{4,6},{5,7},{6,0},{7,1},{8,10},{9,11},{10,... | collective-permute-start | bytes 1179656 | tf_op jit(solution)/shard_map/ppermute | solution.py:400
  133.2 25.1 %copy-start.3 = (s32[8,64]{1,0:T(8,128)S(1)}, s32[8,64]{1,0:T(8,128)}, u32[]{:S(2)}) copy-start(s32[8,64]{1,0:T(8,128)} %param.9) | copy-start | bytes 6148
  133.2 34.1 %copy-start = (bf16[8,64,2048]{2,1,0:T(8,128)(2,1)S(1)}, bf16[8,64,2048]{2,1,0:T(8,128)(2,1)}, u32[]{:S(2)}) copy-start(bf16[8,64,2048]{2,1,0:T(8,128)(2,1)} %param.6) | copy-start | bytes 6291460
  133.2 16.5 %collective-permute-start.9 = (bf16[12,16,1024]{2,1,0:T(8,128)(2,1)S(1)}, bf16[12,16,1024]{2,1,0:T(8,128)(2,1)S(1)}, u32[]{:S(2)}, u32[]{:S(2)}) collective-permute-start(bf16[12,16,1024]{2,1,0:T(8,128)(2,1)S(1)} %get-tuple-element.34), channel_id=1, source_target_pairs={{0,2},{1,3},{2,4},{3,5},{4,6},{5,7},{6,0},{7,1},{8,10},{9,11},{10,... | collective-permute-start | bytes 1179656 | tf_op jit(solution)/shard_map/ppermute | solution.py:400
  134.1 15.6 %collective-permute-start.8 = (bf16[12,16,1024]{2,1,0:T(8,128)(2,1)S(1)}, bf16[12,16,1024]{2,1,0:T(8,128)(2,1)S(1)}, u32[]{:S(2)}, u32[]{:S(2)}) collective-permute-start(bf16[12,16,1024]{2,1,0:T(8,128)(2,1)S(1)} %add_convert_fusion.2), channel_id=1, source_target_pairs={{0,6},{1,7},{2,0},{3,1},{4,2},{5,3},{6,4},{7,5},{8,14},{9,15},{10,... | collective-permute-start | bytes 1179656 | tf_op jit(solution)/shard_map/ppermute | solution.py:400
  142.9 9.8 %collective-permute-start.13 = (bf16[12,16,1024]{2,1,0:T(8,128)(2,1)S(1)}, bf16[12,16,1024]{2,1,0:T(8,128)(2,1)S(1)}, u32[]{:S(2)}, u32[]{:S(2)}) collective-permute-start(bf16[12,16,1024]{2,1,0:T(8,128)(2,1)S(1)} %add_convert_fusion), channel_id=1, source_target_pairs={{0,1},{1,0},{2,3},{3,2},{4,5},{5,4},{6,7},{7,6},{8,9},{9,8},{10,11... | collective-permute-start | bytes 1179656 | tf_op jit(solution)/shard_map/ppermute | solution.py:400
  154.6 12.8 %all-to-all-start.3 = ((bf16[16,12,8,128]{3,2,1,0:T(8,128)(2,1)}), bf16[16,12,8,128]{3,2,1,0:T(8,128)(2,1)S(1)}, u32[]{:S(2)}, u32[]{:S(2)}) async-start(bf16[16,12,8,128]{3,2,1,0:T(8,128)(2,1)} %fold.1), calls=%async_computation.3 | async-start | bytes 786432 | tf_op jit(solution)/shard_map/all_to_all | solution.py:408
  167.4 1.4 copy-start.2
where the time goes:
time: 173 us; the launch traced here: 172 us
  waiting for transfers between devices  59 us (34%)
  Pallas kernels  43.2 us (25%)
  starting transfers between devices  33.8 us (20%)
  blocking collectives  30.6 us (18%)
  local copies, waits for them, and re-layouts  4.36 us (3%)
    ppermute x14, waiting for transfers between devices, shift(): return lax.ppermute(value, 'src', pairs)  36.7 us
    all_to_all x2, blocking collectives, exchange(): lax.all_to_all(value, 'freq', split_axis=0, concat_axis=0, tiled=True)  30.6 us
    ppermute x14, starting transfers between devices, shift(): return lax.ppermute(value, 'src', pairs)  26.5 us
    all_to_all x2, waiting for transfers between devices, exchange(): lax.all_to_all(value, 'freq', split_axis=0, concat_axis=0, tiled=True)  22.3 us
    all_to_all x2, starting transfers between devices, exchange(): lax.all_to_all(value, 'freq', split_axis=0, concat_axis=0, tiled=True)  7.32 us
    pallas_call x1, Pallas kernels, truncate(): pl.pallas_call(truncate_body, grid=(UP_POINTS,), in_specs=[pl.BlockSpec((...  6.88 us
    pallas_call x1, Pallas kernels, forward(): pl.pallas_call(forward_body, in_specs=[SMEM_SPEC] + [VMEM_SPEC] * (len(bl...  6.28 us
    pallas_call x1, Pallas kernels, spectrum(): pl.pallas_call(spectrum_body, grid=(count // tile,), in_specs=[pl.BlockSp...  6.04 us
  transfers between devices with their start and end apart: 16, of which 11 were waited for; matrix products, arithmetic and copies ran while one was open for 0% of the time, Pallas kernels for 8%

commit v1 on v0

v1 whole, which is shorter than its diff:
```python
import functools
import math

import jax
import jax.numpy as jnp
from jax import lax
from jax.experimental import pallas as pl
from jax.experimental.pallas import tpu as pltpu
from jax.sharding import PartitionSpec as P


NT = 2048
NF = 192
BIN0 = 16
NFREQ = 16
NSRC = 8
NY = 4
J = NF // NFREQ
BANDS = 2
J2 = J // BANDS
ROWS = 2 * NF // BANDS
WIDE = 4 * ROWS
PART = WIDE // NFREQ
HT = NT // 2
POINTS = 8
UP_POINTS = 4
RECV = 64
R = NFREQ * RECV
SOURCES = 256
SCALE = 2.0 / NT
F32 = jnp.float32
BF16 = jnp.bfloat16


NT_DIMS = (((1,), (1,)), ((), ()))
TN_DIMS = (((0,), (0,)), ((), ()))

OWN, UP, DOWN, FAR, ACROSS, ACROSS_UP, ACROSS_DOWN, ACROSS_FAR = range(8)
RELATIVE = ((0, 0), (3, 0), (1, 0), (2, 0), (0, 1), (3, 1), (1, 1), (2, 1))
NEAR = (OWN, UP, DOWN, ACROSS)
REMOTE = (FAR, ACROSS_UP, ACROSS_DOWN, ACROSS_FAR)


VMEM_SPEC = pl.BlockSpec(memory_space=pltpu.VMEM)
SMEM_SPEC = pl.BlockSpec(memory_space=pltpu.SMEM)
HBM_SPEC = pl.BlockSpec(memory_space=pltpu.HBM)


def params(limit=24):
    return pltpu.CompilerParams(
        dimension_semantics=("arbitrary",), vmem_limit_bytes=limit << 20
    )


def cost(flops, bytes_accessed):
    return pl.CostEstimate(flops=flops, bytes_accessed=bytes_accessed, transcendentals=0)


def turn(phase):
    quarter = (phase + NT // 8) >> 9
    rest = (phase - (quarter << 9)).astype(F32) * (2.0 * math.pi / NT)
    square = rest * rest
    sine = rest * (
        1.0 + square * (-1.0 / 6 + square * (1.0 / 120 + square * (-1.0 / 5040 + square / 362880)))
    )
    cosine = 1.0 + square * (
        -0.5 + square * (1.0 / 24 + square * (-1.0 / 720 + square * (1.0 / 40320 - square / 3628800)))
    )
    odd = (quarter & 1) == 1
    first, second = jnp.where(odd, sine, cosine), jnp.where(odd, cosine, sine)
    behind = ((quarter + 1) & 2) == 2
    below = (quarter & 2) == 2
    return jnp.where(behind, -first, first), jnp.where(below, -second, second)


def write_table(table):
    lane = lax.broadcasted_iota(jnp.int32, (ROWS, 128), 1)
    row = lax.broadcasted_iota(jnp.int32, (ROWS, 128), 0)
    quarter = row & 1
    for parity in range(BANDS):
        bin_index = BIN0 + parity + row - quarter
        fine_cos, fine_sin = turn((lane * bin_index) & (NT - 1))
        coarse_cos, coarse_sin = turn(((lane * bin_index + 4 * quarter) & 15) << 7)
        for a in range(HT // 128):
            value = coarse_cos[:, a : a + 1] * fine_cos - coarse_sin[:, a : a + 1] * fine_sin
            table[parity, :, a * 128 : (a + 1) * 128] = value.astype(BF16)


def forward_bands(table, early, late):
    for parity, mixed in enumerate((early + late, early - late)):
        yield parity, lax.dot_general(
            table[parity], mixed.astype(BF16), NT_DIMS, preferred_element_type=F32
        )


def inverse_bands(table, bands):
    even, odd = [
        lax.dot_general(bands[p], table[p], TN_DIMS, preferred_element_type=F32)
        for p in range(BANDS)
    ]
    return (even + odd) * SCALE, (even - odd) * SCALE


def spectrum_body(traces, table, out, wide):
    step = pl.program_id(0)

    @pl.when(step == 0)
    def _():
        write_table(table)

    rows = traces[...].reshape(2 * RECV, NT).astype(F32)
    for parity, bins in forward_bands(table, rows[:, :HT], rows[:, HT:]):
        wide.at[parity][pl.ds(step, ROWS, stride=UP_POINTS), :] = bins

    @pl.when(step == pl.num_programs(0) - 1)
    def _():
        for parity in range(BANDS):
            for f in range(NFREQ):
                out[f, parity] = wide[parity, f * PART : f * PART + PART].astype(BF16)


def spectrum(traces):
    return pl.pallas_call(
        spectrum_body,
        grid=(UP_POINTS,),
        in_specs=[pl.BlockSpec((2, 1, RECV, NT), lambda i: (0, i, 0, 0))],
        out_specs=[
            pl.BlockSpec((BANDS, ROWS, HT), lambda i: (0, 0, 0)),
            pl.BlockSpec((NFREQ, BANDS, PART, 128), lambda i: (0, 0, 0, 0)),
        ],
        out_shape=[
            jax.ShapeDtypeStruct((BANDS, ROWS, HT), BF16),
            jax.ShapeDtypeStruct((NFREQ, BANDS, PART, 128), BF16),
        ],
        scratch_shapes=[pltpu.VMEM((BANDS, WIDE, 128), F32)],
        compiler_params=params(),
        cost_estimate=cost(POINTS * RECV * NT * 2 * ROWS, 4 << 20),
        name="spectrum",
    )(traces)


def unfold_body(bins, out):
    low = lax.broadcasted_iota(jnp.int32, (8, 128), 1) < RECV

    def step(j, carry):
        for pair in range(NFREQ // 2):
            even = bins[2 * pair, j].astype(F32)
            odd = bins[2 * pair + 1, j].astype(F32)
            first = jnp.where(low, even, pltpu.roll(odd, RECV, 1))
            second = jnp.where(low, pltpu.roll(even, RECV, 1), odd)
            both = jnp.concatenate([first, second], axis=0).astype(BF16)
            out[j, :, pair * 128 : pair * 128 + 128] = both
        return carry

    lax.fori_loop(0, J, step, 0)


def unfold(bins):
    return pl.pallas_call(
        unfold_body,
        in_specs=[VMEM_SPEC],
        out_specs=VMEM_SPEC,
        out_shape=jax.ShapeDtypeStruct((J, 2 * POINTS, R), BF16),
        compiler_params=pltpu.CompilerParams(vmem_limit_bytes=8 << 20),
        cost_estimate=cost(0, 1 << 20),
        name="unfold",
    )(bins)


def swapped(value, sign):
    rows, lanes = value.shape
    tiles = value.reshape(rows // 8, 2, 4, lanes)
    return jnp.concatenate([-sign * tiles[:, 1:], sign * tiles[:, :1]], axis=1).reshape(rows, lanes)


def places(me):
    y, z = me // 2, me % 2
    return [2 * ((y + dy) % NY) + (z + dz) % 2 for dy, dz in RELATIVE]


def hold_body(kern, held, sems):
    copies = [
        pltpu.make_async_copy(kern.at[part], held.at[part], sems.at[part]) for part in range(2)
    ]
    for copy in copies:
        copy.start()
    for copy in copies:
        copy.wait()


def hold(kern):
    return pl.pallas_call(
        hold_body,
        in_specs=[HBM_SPEC],
        out_specs=pl.BlockSpec(memory_space=pl.ANY),
        out_shape=pltpu.VMEM(kern.shape, BF16),
        scratch_shapes=[pltpu.SemaphoreType.DMA((2,))],
        compiler_params=pltpu.CompilerParams(vmem_limit_bytes=1 << 20),
        cost_estimate=cost(0, 13 << 20),
        name="hold",
    )(kern)


def forward_body(me, *refs):
    *blocks, kern, out = refs
    place = places(me[0])

    def step(j2, carry):
        for parity in range(BANDS):
            j = parity * J2 + j2
            at = BANDS * j2 + parity
            field = jnp.concatenate([b[j] for b in blocks], axis=0)
            by_real = lax.dot_general(field, kern[0, at], NT_DIMS, preferred_element_type=F32)
            by_imag = lax.dot_general(field, kern[1, at], NT_DIMS, preferred_element_type=F32)
            waves = (by_real + swapped(by_imag, 1.0)).astype(BF16).reshape(NSRC, 2, 8, SOURCES)
            for rel in range(NSRC):
                for half in range(2):
                    out[2 * place[rel] + half, j] = waves[rel, half]
        return carry

    lax.fori_loop(0, J2, step, 0)


def forward(me, blocks, kern):
    return pl.pallas_call(
        forward_body,
        in_specs=[SMEM_SPEC] + [VMEM_SPEC] * (NSRC + 1),
        out_specs=VMEM_SPEC,
        out_shape=jax.ShapeDtypeStruct((NFREQ, J, 8, SOURCES), BF16),
        compiler_params=pltpu.CompilerParams(vmem_limit_bytes=8 << 20),
        cost_estimate=cost(8 * J * 64 * SOURCES * R, 4 << 20),
        name="forward",
    )(me, *blocks, kern)


def terms_of(place, field_ref, held, which, outs, j2, parity):
    j = parity * J2 + j2
    at = BANDS * j2 + parity
    field = jnp.concatenate(
        [field_ref[2 * place[rel] + half, j] for rel in which for half in range(2)], axis=0
    )
    by_real = jnp.dot(field, held[0, at], preferred_element_type=F32)
    by_imag = jnp.dot(field, held[1, at], preferred_element_type=F32)
    terms = (by_real + swapped(by_imag, -1.0)).astype(BF16)
    for index in range(len(which)):
        outs[index][j] = terms[index * 16 : index * 16 + 16]


def adjoint_remote_body(me, field_ref, kern, *refs):
    *outs, held, sems = refs
    place = places(me[0])

    def copies(at):
        return [
            pltpu.make_async_copy(kern.at[part, at], held.at[part, at], sems.at[part, at])
            for part in range(2)
        ]

    for at in range(J):
        for copy in copies(at):
            copy.start()

    def step(j2, carry):
        for parity in range(BANDS):
            for copy in copies(BANDS * j2 + parity):
                copy.wait()
            terms_of(place, field_ref, held, REMOTE, outs, j2, parity)
        return carry

    lax.fori_loop(0, J2, step, 0)


def adjoint_remote(me, field, kern):
    term = jax.ShapeDtypeStruct((J, 2 * POINTS, R), BF16)
    *terms, held = pl.pallas_call(
        adjoint_remote_body,
        in_specs=[SMEM_SPEC, VMEM_SPEC, HBM_SPEC],
        out_specs=[VMEM_SPEC] * (len(REMOTE) + 1),
        out_shape=[term] * len(REMOTE) + [pltpu.VMEM(kern.shape, BF16)],
        scratch_shapes=[pltpu.SemaphoreType.DMA((2, J))],
        compiler_params=pltpu.CompilerParams(vmem_limit_bytes=8 << 20),
        cost_estimate=cost(4 * J * 64 * SOURCES * R, 14 << 20),
        name="adjoint_remote",
    )(me, field, kern)
    return terms, held


def adjoint_near_body(me, field_ref, held, *outs):
    place = places(me[0])

    def step(j2, carry):
        for parity in range(BANDS):
            terms_of(place, field_ref, held, NEAR, outs, j2, parity)
        return carry

    lax.fori_loop(0, J2, step, 0)


def adjoint_near(me, field, held):
    return pl.pallas_call(
        adjoint_near_body,
        in_specs=[SMEM_SPEC, VMEM_SPEC, VMEM_SPEC],
        out_specs=[VMEM_SPEC] * len(NEAR),
        out_shape=[jax.ShapeDtypeStruct((J, 2 * POINTS, R), BF16)] * len(NEAR),
        compiler_params=pltpu.CompilerParams(vmem_limit_bytes=8 << 20),
        cost_estimate=cost(4 * J * 64 * SOURCES * R, 2 << 20),
        name="adjoint_near",
    )(me, field, held)


def fold_body(*refs):
    *terms, out = refs
    low = lax.broadcasted_iota(jnp.int32, (8, 128), 1) < RECV

    def step(j, carry):
        total = functools.reduce(lambda a, b: a + b, [t[j].astype(F32) for t in terms])
        for pair in range(NFREQ // 2):
            first = total[:8, pair * 128 : pair * 128 + 128]
            second = total[8:, pair * 128 : pair * 128 + 128]
            out[2 * pair, j] = jnp.where(low, first, pltpu.roll(second, RECV, 1)).astype(BF16)
            out[2 * pair + 1, j] = jnp.where(low, pltpu.roll(first, RECV, 1), second).astype(BF16)
        return carry

    lax.fori_loop(0, J, step, 0)


def fold(terms):
    return pl.pallas_call(
        fold_body,
        in_specs=[VMEM_SPEC] * len(terms),
        out_specs=VMEM_SPEC,
        out_shape=jax.ShapeDtypeStruct((NFREQ, J, 8, 128), BF16),
        compiler_params=pltpu.CompilerParams(vmem_limit_bytes=8 << 20),
        cost_estimate=cost(0, 2 << 20),
        name="fold",
    )(*terms)


LANES = [slice(half * 128, half * 128 + 128) for half in range(SOURCES // 128)]


def parts():
    for parity in range(BANDS):
        for f in range(NFREQ):
            start = (f * BANDS + parity) * PART
            yield parity, slice(f * PART, f * PART + PART), slice(start, start + PART)


def truncate_body(waves, table, onset, up, back, wide_in, wide_out):
    step = pl.program_id(0)

    @pl.when(step == 0)
    def _():
        for parity, inner, outer in parts():
            for half, lanes in enumerate(LANES):
                wide_in[parity, half, inner] = waves[outer, lanes].astype(F32)

    every = pl.ds(step, ROWS, stride=UP_POINTS)
    bands = [
        jnp.concatenate(
            [wide_in.at[parity, half][every, :] for half in range(len(LANES))], axis=1
        ).astype(BF16)
        for parity in range(BANDS)
    ]
    limit = onset[pl.ds(step, 1), :].astype(F32)
    limit = jnp.broadcast_to(limit, (128, SOURCES)).T[:, :1].astype(jnp.int32)
    sample = lax.broadcasted_iota(jnp.int32, (SOURCES, HT), 1)
    kept = []
    for half, signal in enumerate(inverse_bands(table, bands)):
        kept.append(jnp.where(sample < limit - half * HT, signal, 0.0).astype(BF16))
        up[:, half * HT : half * HT + HT] = kept[-1]
    for parity, bins in forward_bands(table, kept[0].astype(F32), kept[1].astype(F32)):
        for half, lanes in enumerate(LANES):
            wide_out.at[parity, half][every, :] = bins[:, lanes]

    @pl.when(step == pl.num_programs(0) - 1)
    def _():
        for parity, inner, outer in parts():
            for half, lanes in enumerate(LANES):
                back[outer, lanes] = wide_out[parity, half, inner].astype(BF16)


def truncate(waves, table, onset):
    rows = waves.shape[0]
    return pl.pallas_call(
        truncate_body,
        grid=(UP_POINTS,),
        in_specs=[
            pl.BlockSpec((rows, SOURCES), lambda i: (0, 0)),
            pl.BlockSpec((BANDS, ROWS, HT), lambda i: (0, 0, 0)),
            pl.BlockSpec((UP_POINTS, SOURCES), lambda i: (0, 0)),
        ],
        out_specs=[
            pl.BlockSpec((SOURCES, NT), lambda i: (i, 0)),
            pl.BlockSpec((rows, SOURCES), lambda i: (0, 0)),
        ],
        out_shape=[
            jax.ShapeDtypeStruct((UP_POINTS * SOURCES, NT), BF16),
            jax.ShapeDtypeStruct((rows, SOURCES), BF16),
        ],
        scratch_shapes=[pltpu.VMEM((BANDS, len(LANES), WIDE, 128), F32)] * 2,
        compiler_params=params(),
        cost_estimate=cost(2 * UP_POINTS * SOURCES * NT * 2 * ROWS, 8 << 20),
        name="truncate",
    )(waves, table, onset)


def update_body(bins, table, direct, onset, out, wide):
    step = pl.program_id(0)

    @pl.when(step == 0)
    def _():
        for parity, inner, outer in parts():
            wide[parity, inner] = bins[outer, :].astype(F32)

    every = pl.ds(step, ROWS, stride=UP_POINTS)
    bands = [wide.at[parity][every, :].astype(BF16) for parity in range(BANDS)]
    limit = onset[...].reshape(2 * RECV, 1)
    sample = lax.broadcasted_iota(jnp.int32, (2 * RECV, HT), 1)
    for half, trace in enumerate(inverse_bands(table, bands)):
        span = slice(half * HT, half * HT + HT)
        cut = jnp.where(sample < limit - half * HT, trace, 0.0)
        before = direct[:, 0, :, span].reshape(2 * RECV, HT).astype(F32)
        out[:, 0, :, span] = (before - cut).astype(BF16).reshape(2, RECV, HT)


def update(bins, table, direct, onset):
    rows = bins.shape[0]
    return pl.pallas_call(
        update_body,
        grid=(UP_POINTS,),
        in_specs=[
            pl.BlockSpec((rows, 2 * RECV), lambda i: (0, 0)),
            pl.BlockSpec((BANDS, ROWS, HT), lambda i: (0, 0, 0)),
            pl.BlockSpec((2, 1, RECV, NT), lambda i: (0, i, 0, 0)),
            pl.BlockSpec((2, 1, RECV, 1), lambda i: (0, i, 0, 0)),
        ],
        out_specs=pl.BlockSpec((2, 1, RECV, NT), lambda i: (0, i, 0, 0)),
        out_shape=jax.ShapeDtypeStruct((2, UP_POINTS, RECV, NT), BF16),
        scratch_shapes=[pltpu.VMEM((BANDS, WIDE, 2 * RECV), F32)],
        compiler_params=params(),
        cost_estimate=cost(POINTS * RECV * NT * 2 * ROWS, 5 << 20),
        name="update",
    )(bins, table, direct, onset)


def shift(value, dy, dz):
    pairs = [
        (2 * y + z, 2 * ((y + dy) % NY) + (z + dz) % 2) for y in range(NY) for z in range(2)
    ]
    return lax.ppermute(value, "src", pairs)


def add(*terms):
    return functools.reduce(lambda a, b: a + b, [t.astype(F32) for t in terms]).astype(BF16)


def exchange(value):
    return lax.all_to_all(value, "freq", split_axis=0, concat_axis=0, tiled=True)


def whole(focusing, direct, kernel, onset_up, onset_back):
    me = lax.axis_index("src").reshape(1)
    back_onset = onset_back.reshape(2, UP_POINTS, RECV, 1)
    kernel = pltpu.with_memory_space_constraint(kernel, pltpu.HBM)

    traces = focusing.reshape(2, UP_POINTS, RECV, NT)
    table, bins = spectrum(pltpu.with_memory_space_constraint(traces, pltpu.HBM))
    bins, me, back_onset = lax.optimization_barrier((bins, me, back_onset))
    own = unfold(exchange(bins).reshape(NFREQ, J, 8, 128))
    own, late_kernel = lax.optimization_barrier((own, kernel))

    across = shift(own, 0, 1)
    up = shift(own, 1, 0)
    down = shift(own, -1, 0)
    held = hold(pltpu.with_memory_space_constraint(late_kernel, pltpu.HBM))
    across_down = shift(across, -1, 0)
    across_up = shift(across, 1, 0)
    far = shift(up, 1, 0)
    across_far = shift(across_down, -1, 0)
    blocks = [own, up, down, far, across, across_up, across_down, across_far]
    waves = exchange(forward(me, blocks, held))

    upgoing, back = truncate(waves.reshape(NFREQ * J * 8, SOURCES), table, onset_up)
    back = exchange(back.reshape(NFREQ, J, 8, SOURCES))

    (far, across_up, across_down, across_far), held = adjoint_remote(me, back, kernel)
    own, up, down, across = adjoint_near(me, back, held)
    r1 = shift(across_far, 1, 0)
    r5 = shift(far, -1, 0)
    r3 = shift(across_up, -1, 0)
    r2 = shift(add(across_down, r1), 1, 0)
    r6 = shift(add(up, r5), -1, 0)
    r4 = shift(add(across, r2, r3), 0, 1)
    r7 = shift(down, 1, 0)
    summed = exchange(fold([own, r6, r7, r4]))

    updated = update(
        summed.reshape(NFREQ * J * 8, 2 * RECV),
        table,
        direct.reshape(2, UP_POINTS, RECV, NT),
        back_onset,
    )
    return (
        upgoing.reshape(UP_POINTS, SOURCES, NT),
        updated.reshape(POINTS, RECV, NT),
    )


def solution(mesh):
    placed = (
        P("src", "freq", None),
        P("src", "freq", None),
        P(None, "freq", "src", None),
        P("freq", "src"),
        P("src", "freq"),
    )
    return jax.shard_map(
        whole,
        mesh=mesh,
        in_specs=placed,
        out_specs=(P("freq", "src", None), P("src", "freq", None)),
        check_vma=False,
    )
```

time: 173 us -> 166 us (0.960)
  blocking collectives: 30.6 us -> 46.8 us
  Pallas kernels: 43.2 us -> 34.7 us
  waiting for transfers between devices: 59 us -> 51.4 us
  local copies, waits for them, and re-layouts: 4.36 us -> 0.17 us
  starting transfers between devices: 33.8 us -> 30.3 us
    all_to_all x2 -> x3, blocking collectives: 30.6 us -> 46.8 us  [exchange(): lax.all_to_all(value, 'freq', split_axis=0, concat_axis=0, tiled=True)]
    all_to_all x2 -> x1, waiting for transfers between devices: 22.3 us -> 8.91 us  [exchange(): lax.all_to_all(value, 'freq', split_axis=0, concat_axis=0, tiled=True)]
    pallas_call x3, Pallas kernels: 17.7 us -> 10.6 us  [the longest x1 5.07 us: forward(): pl.pallas_call(forward_body, in_specs=[SMEM_SPEC] + [VMEM_SPEC] * (NSRC +...]
    ppermute x14, waiting for transfers between devices: 36.7 us -> 42.5 us  [shift(): return lax.ppermute(value, 'src', pairs)]
    all_to_all x2 -> x1, starting transfers between devices: 7.32 us -> 3.71 us  [exchange(): lax.all_to_all(value, 'freq', split_axis=0, concat_axis=0, tiled=True)]
    unnamed x9 -> x6, local copies, waits for them, and re-layouts: 2.15 us -> 0.02 us
  transfers between devices with their start and end apart: 16 -> 15, of which waited for: 11 -> 11; matrix products, arithmetic and copies ran while one was open for 0% -> 0% of each run, Pallas kernels for 8% -> 5%
where the time goes in v1:
time: 166 us; the launch traced here: 165 us
  waiting for transfers between devices  51.4 us (31%)
  blocking collectives  46.8 us (28%)
  Pallas kernels  34.7 us (21%)
  starting transfers between devices  30.3 us (18%)
    all_to_all x3, blocking collectives, exchange(): lax.all_to_all(value, 'freq', split_axis=0, concat_axis=0, tiled=True)  46.8 us
    ppermute x14, waiting for transfers between devices, shift(): return lax.ppermute(value, 'src', pairs)  42.5 us
    ppermute x14, starting transfers between devices, shift(): return lax.ppermute(value, 'src', pairs)  26.6 us
    all_to_all x1, waiting for transfers between devices, exchange(): lax.all_to_all(value, 'freq', split_axis=0, concat_axis=0, tiled=True)  8.91 us
    pallas_call x1, Pallas kernels, truncate(): pl.pallas_call(truncate_body, grid=(UP_POINTS,), in_specs=[pl.BlockSpec((...  6.17 us
    pallas_call x1, Pallas kernels, adjoint_remote(): pl.pallas_call(adjoint_remote_body, in_specs=[SMEM_SPEC, VMEM_SPEC, HBM_S...  5.11 us
    pallas_call x1, Pallas kernels, forward(): pl.pallas_call(forward_body, in_specs=[SMEM_SPEC] + [VMEM_SPEC] * (NSRC +...  5.07 us
    pallas_call x1, Pallas kernels, hold(): pl.pallas_call(hold_body, in_specs=[HBM_SPEC], out_specs=pl.BlockSpec(mem...  4.62 us
  transfers between devices with their start and end apart: 15, of which 11 were waited for; matrix products, arithmetic and copies ran while one was open for 0% of the time, Pallas kernels for 5%

profile of v1, /device:TPU:0, one launch (start us, length us, event | category | flops | bytes accessed | tf_op | source)
XLA Modules:
  0.0 164.5 jit_solution(2061365393391415341)
XLA Ops:
  0.6 4.6 %spectrum.1 = (bf16[2,192,1024]{2,1,0:T(8,128)(2,1)S(1)}, bf16[16,2,48,128]{3,2,1,0:T(8,128)(2,1)S(1)}) custom-call(bf16[2,4,64,2048]{3,2,1,0:T(8,128)(2,1)} %bitcast.15), custom_call_target="tpu_custom_call" | custom-call | flops 402653184 | bytes 4194304 | tf_op jit(solution)/shard_map/spectrum/pallas_call | solution.py:123
  5.2 14.7 %all_to_all.20 = bf16[16,2,48,128]{3,2,1,0:T(8,128)(2,1)S(1)} all-to-all(bf16[16,2,48,128]{3,2,1,0:T(8,128)(2,1)S(1)} %get-tuple-element.22), channel_id=1, replica_groups=mesh['freq'=16,'src'=8] {'freq'}, dimensions={0} | all-to-all | bytes 786432 | tf_op jit(solution)/shard_map/all_to_all | solution.py:459
  21.0 3.7 %collective-permute-start.3 = (bf16[12,16,1024]{2,1,0:T(8,128)(2,1)S(1)}, bf16[12,16,1024]{2,1,0:T(8,128)(2,1)S(1)}, u32[]{:S(2)}, u32[]{:S(2)}) collective-permute-start(bf16[12,16,1024]{2,1,0:T(8,128)(2,1)S(1)} %unfold.1.refs_0_), channel_id=1, source_target_pairs={{0,1},{1,0},{2,3},{3,2},{4,5},{5,4},{6,7},{7,6},{8,9},{9,8},{10,11... | collective-permute-start | bytes 1179656 | tf_op jit(solution)/shard_map/ppermute | solution.py:451
  24.6 1.6 collective-permute-start
  26.2 7.6 %collective-permute-done.3.refs_4_ = bf16[12,16,1024]{2,1,0:T(8,128)(2,1)S(1)} collective-permute-done((bf16[12,16,1024]{2,1,0:T(8,128)(2,1)S(1)}, bf16[12,16,1024]{2,1,0:T(8,128)(2,1)S(1)}, u32[]{:S(2)}, u32[]{:S(2)}) %collective-permute-start.3) | collective-permute-done | bytes 393248 | tf_op jit(solution)/shard_map/ppermute | solution.py:451
  33.8 3.0 %collective-permute-start.5 = (bf16[12,16,1024]{2,1,0:T(8,128)(2,1)S(1)}, bf16[12,16,1024]{2,1,0:T(8,128)(2,1)S(1)}, u32[]{:S(2)}, u32[]{:S(2)}) collective-permute-start(bf16[12,16,1024]{2,1,0:T(8,128)(2,1)S(1)} %collective-permute-done.3.refs_4_), channel_id=1, source_target_pairs={{0,6},{1,7},{2,0},{3,1},{4,2},{5,3},{6,4},{7,5},{8,14},{9,15},{10,... | collective-permute-start | bytes 1179656 | tf_op jit(solution)/shard_map/ppermute | solution.py:451
  37.6 1.3 collective-permute-start.4
  38.9 7.5 %collective-permute-done.5.refs_6_ = bf16[12,16,1024]{2,1,0:T(8,128)(2,1)S(1)} collective-permute-done((bf16[12,16,1024]{2,1,0:T(8,128)(2,1)S(1)}, bf16[12,16,1024]{2,1,0:T(8,128)(2,1)S(1)}, u32[]{:S(2)}, u32[]{:S(2)}) %collective-permute-start.5) | collective-permute-done | bytes 393248 | tf_op jit(solution)/shard_map/ppermute | solution.py:451
  46.3 3.7 %collective-permute-start.6 = (bf16[12,16,1024]{2,1,0:T(8,128)(2,1)S(1)}, bf16[12,16,1024]{2,1,0:T(8,128)(2,1)S(1)}, u32[]{:S(2)}, u32[]{:S(2)}) collective-permute-start(bf16[12,16,1024]{2,1,0:T(8,128)(2,1)S(1)} %collective-permute-done.5.refs_6_), channel_id=1, source_target_pairs={{0,6},{1,7},{2,0},{3,1},{4,2},{5,3},{6,4},{7,5},{8,14},{9,15},{10,... | collective-permute-start | bytes 1179656 | tf_op jit(solution)/shard_map/ppermute | solution.py:451
  50.0 4.6 %hold.1.refs_8_ = bf16[2,12,256,1024]{3,2,1,0:T(8,128)(2,1)S(1)} custom-call(bf16[2,12,256,1024]{3,2,1,0:T(8,128)(2,1)} %kern.2), custom_call_target="tpu_custom_call" | custom-call | bytes 13631488 | tf_op jit(solution)/shard_map/hold/pallas_call | solution.py:192
  54.8 2.3 %collective-permute-done.2.refs_3_ = bf16[12,16,1024]{2,1,0:T(8,128)(2,1)S(1)} collective-permute-done((bf16[12,16,1024]{2,1,0:T(8,128)(2,1)S(1)}, bf16[12,16,1024]{2,1,0:T(8,128)(2,1)S(1)}, u32[]{:S(2)}, u32[]{:S(2)}) %collective-permute-start.2) | collective-permute-done | bytes 393248 | tf_op jit(solution)/shard_map/ppermute | solution.py:451
  57.0 4.6 %collective-permute-done.6.refs_7_ = bf16[12,16,1024]{2,1,0:T(8,128)(2,1)S(1)} collective-permute-done((bf16[12,16,1024]{2,1,0:T(8,128)(2,1)S(1)}, bf16[12,16,1024]{2,1,0:T(8,128)(2,1)S(1)}, u32[]{:S(2)}, u32[]{:S(2)}) %collective-permute-start.6) | collective-permute-done | bytes 393248 | tf_op jit(solution)/shard_map/ppermute | solution.py:451
  61.6 5.1 %forward.1 = bf16[16,12,8,256]{3,2,1,0:T(8,128)(2,1)S(1)} custom-call(s32[1]{0:T(128)} %bitcast.1.me, bf16[12,16,1024]{2,1,0:T(8,128)(2,1)S(1)} %unfold.1.refs_0_, bf16[12,16,1024]{2,1,0:T(8,128)(2,1)S(1)} %collective-permute-done.refs_1_, bf16[12,16,1024]{2,1,0:T(8,128)(2,1)S(1)} %collective-permute-done.1.refs_2_, ...), custom_call_target="tpu_custom_call" | custom-call | flops 1610612736 | bytes 4194304 | tf_op jit(solution)/shard_map/forward/pallas_call | solution.py:225
  66.7 16.1 %all_to_all.21 = bf16[16,12,8,256]{3,2,1,0:T(8,128)(2,1)S(1)} all-to-all(bf16[16,12,8,256]{3,2,1,0:T(8,128)(2,1)S(1)} %forward.1), channel_id=1, replica_groups=mesh['freq'=16,'src'=8] {'freq'}, dimensions={0} | all-to-all | bytes 1572864 | tf_op jit(solution)/shard_map/all_to_all | solution.py:459
  82.8 6.2 %truncate.1 = (bf16[1024,2048]{1,0:T(8,128)(2,1)}, bf16[1536,256]{1,0:T(8,128)(2,1)S(1)}) custom-call(bf16[1536,256]{1,0:T(8,128)(2,1)S(1)} %bitcast.13, bf16[2,192,1024]{2,1,0:T(8,128)(2,1)S(1)} %get-tuple-element.25.table, s32[4,256]{1,0:T(4,128)S(1)} %copy-done.1), custom_call_target="tpu_custom_call" | custom-call | flops 1610612736 | bytes 8388608 | tf_op jit(solution)/shard_map/truncate/pallas_call | solution.py:385
  89.0 15.9 %all_to_all.22.field_ref = bf16[16,12,8,256]{3,2,1,0:T(8,128)(2,1)S(1)} all-to-all(bf16[16,12,8,256]{3,2,1,0:T(8,128)(2,1)S(1)} %bitcast.14), channel_id=1, replica_groups=mesh['freq'=16,'src'=8] {'freq'}, dimensions={0} | all-to-all | bytes 1572864 | tf_op jit(solution)/shard_map/all_to_all | solution.py:459
  104.8 5.1 %adjoint_remote.1 = (bf16[12,16,1024]{2,1,0:T(8,128)(2,1)S(1)}, bf16[12,16,1024]{2,1,0:T(8,128)(2,1)S(1)}, bf16[12,16,1024]{2,1,0:T(8,128)(2,1)S(1)}, bf16[12,16...) custom-call(s32[1]{0:T(128)} %bitcast.1.me, bf16[16,12,8,256]{3,2,1,0:T(8,128)(2,1)S(1)} %all_to_all.22.field_ref, ...), custom_call_target="tpu_custom_call" | custom-call | flops 805306368 | bytes 14680064 | tf_op jit(solution)/shard_map/adjoint_remote/pallas_call | solution.py:275
  110.0 1.1 collective-permute-start.10
  111.1 2.7 %collective-permute-start.7 = (bf16[12,16,1024]{2,1,0:T(8,128)(2,1)S(1)}, bf16[12,16,1024]{2,1,0:T(8,128)(2,1)S(1)}, u32[]{:S(2)}, u32[]{:S(2)}) collective-permute-start(bf16[12,16,1024]{2,1,0:T(8,128)(2,1)S(1)} %get-tuple-element.31), channel_id=1, source_target_pairs={{0,6},{1,7},{2,0},{3,1},{4,2},{5,3},{6,4},{7,5},{8,14},{9,15},{10,... | collective-permute-start | bytes 1179656 | tf_op jit(solution)/shard_map/ppermute | solution.py:451
  113.8 1.9 %collective-permute-start.12 = (bf16[12,16,1024]{2,1,0:T(8,128)(2,1)S(1)}, bf16[12,16,1024]{2,1,0:T(8,128)(2,1)S(1)}, u32[]{:S(2)}, u32[]{:S(2)}) collective-permute-start(bf16[12,16,1024]{2,1,0:T(8,128)(2,1)S(1)} %get-tuple-element.36), channel_id=1, source_target_pairs={{0,6},{1,7},{2,0},{3,1},{4,2},{5,3},{6,4},{7,5},{8,14},{9,15},{10,... | collective-permute-start | bytes 1179656 | tf_op jit(solution)/shard_map/ppermute | solution.py:451
  115.8 7.3 %collective-permute-done.10 = bf16[12,16,1024]{2,1,0:T(8,128)(2,1)S(1)} collective-permute-done((bf16[12,16,1024]{2,1,0:T(8,128)(2,1)S(1)}, bf16[12,16,1024]{2,1,0:T(8,128)(2,1)S(1)}, u32[]{:S(2)}, u32[]{:S(2)}) %collective-permute-start.10) | collective-permute-done | bytes 393248 | tf_op jit(solution)/shard_map/ppermute | solution.py:451
  123.3 3.0 %adjoint_near.1 = (bf16[12,16,1024]{2,1,0:T(8,128)(2,1)S(1)}, bf16[12,16,1024]{2,1,0:T(8,128)(2,1)S(1)}, bf16[12,16,1024]{2,1,0:T(8,128)(2,1)S(1)}, bf16[12,16,1024]{2,1,0:T(8,128)(2,1)S(1)}) custom-call(s32[1]{0:T(128)} %bitcast.1.me, bf16[16,12,8,256]{3,2,1,0:T(8,128)(2,1)S(1)} %all_to_all.22.field_ref, bf16[2,12,256,1024]{3,2,1,0:T(8,128)(2,1)S(1)} %get-tuple-element.28.held), custom_call_target="tpu_custom_call" | custom-call | flops 805306368 | bytes 2097152 | tf_op jit(solution)/shard_map/adjoint_near/pallas_call | solution.py:300
  127.2 2.7 %collective-permute-start.8 = (bf16[12,16,1024]{2,1,0:T(8,128)(2,1)S(1)}, bf16[12,16,1024]{2,1,0:T(8,128)(2,1)S(1)}, u32[]{:S(2)}, u32[]{:S(2)}) collective-permute-start(bf16[12,16,1024]{2,1,0:T(8,128)(2,1)S(1)} %add_convert_fusion.2), channel_id=1, source_target_pairs={{0,6},{1,7},{2,0},{3,1},{4,2},{5,3},{6,4},{7,5},{8,14},{9,15},{10,... | collective-permute-start | bytes 1179656 | tf_op jit(solution)/shard_map/ppermute | solution.py:451
  129.8 1.9 %collective-permute-done.12 = bf16[12,16,1024]{2,1,0:T(8,128)(2,1)S(1)} collective-permute-done((bf16[12,16,1024]{2,1,0:T(8,128)(2,1)S(1)}, bf16[12,16,1024]{2,1,0:T(8,128)(2,1)S(1)}, u32[]{:S(2)}, u32[]{:S(2)}) %collective-permute-start.12) | collective-permute-done | bytes 393248 | tf_op jit(solution)/shard_map/ppermute | solution.py:451
  131.7 4.8 %collective-permute-done.11 = bf16[12,16,1024]{2,1,0:T(8,128)(2,1)S(1)} collective-permute-done((bf16[12,16,1024]{2,1,0:T(8,128)(2,1)S(1)}, bf16[12,16,1024]{2,1,0:T(8,128)(2,1)S(1)}, u32[]{:S(2)}, u32[]{:S(2)}) %collective-permute-start.11) | collective-permute-done | bytes 393248 | tf_op jit(solution)/shard_map/ppermute | solution.py:451
  136.7 3.4 %collective-permute-start.13 = (bf16[12,16,1024]{2,1,0:T(8,128)(2,1)S(1)}, bf16[12,16,1024]{2,1,0:T(8,128)(2,1)S(1)}, u32[]{:S(2)}, u32[]{:S(2)}) collective-permute-start(bf16[12,16,1024]{2,1,0:T(8,128)(2,1)S(1)} %add_convert_fusion), channel_id=1, source_target_pairs={{0,1},{1,0},{2,3},{3,2},{4,5},{5,4},{6,7},{7,6},{8,9},{9,8},{10,11... | collective-permute-start | bytes 1179656 | tf_op jit(solution)/shard_map/ppermute | solution.py:451
  140.1 3.4 %collective-permute-done.9.refs_2_ = bf16[12,16,1024]{2,1,0:T(8,128)(2,1)S(1)} collective-permute-done((bf16[12,16,1024]{2,1,0:T(8,128)(2,1)S(1)}, bf16[12,16,1024]{2,1,0:T(8,128)(2,1)S(1)}, u32[]{:S(2)}, u32[]{:S(2)}) %collective-permute-start.9) | collective-permute-done | bytes 393248 | tf_op jit(solution)/shard_map/ppermute | solution.py:451
  143.5 3.1 %collective-permute-done.13.refs_3_ = bf16[12,16,1024]{2,1,0:T(8,128)(2,1)S(1)} collective-permute-done((bf16[12,16,1024]{2,1,0:T(8,128)(2,1)S(1)}, bf16[12,16,1024]{2,1,0:T(8,128)(2,1)S(1)}, u32[]{:S(2)}, u32[]{:S(2)}) %collective-permute-start.13) | collective-permute-done | bytes 393248 | tf_op jit(solution)/shard_map/ppermute | solution.py:451
  146.5 1.8 %fold.1 = bf16[16,12,8,128]{3,2,1,0:T(8,128)(2,1)} custom-call(bf16[12,16,1024]{2,1,0:T(8,128)(2,1)S(1)} %get-tuple-element.29.refs_0_, bf16[12,16,1024]{2,1,0:T(8,128)(2,1)S(1)} %collective-permute-done.8.refs_1_, bf16[12,16,1024]{2,1,0:T(8,128)(2,1)S(1)} %collective-permute-done.9.refs_2_, bf16[12,16,1024]{2,1,0:T(8,128)(2,1)S(1)} %collective-permute-done.13.refs_3_), custom_call_target="tpu_custom_call" | custom-call | bytes 2097152 | tf_op jit(solution)/shard_map/fold/pallas_call | solution.py:328
  148.4 3.7 %all-to-all-start.3 = ((bf16[16,12,8,128]{3,2,1,0:T(8,128)(2,1)}), bf16[16,12,8,128]{3,2,1,0:T(8,128)(2,1)S(1)}, u32[]{:S(2)}, u32[]{:S(2)}) async-start(bf16[16,12,8,128]{3,2,1,0:T(8,128)(2,1)} %fold.1), calls=%async_computation.3 | async-start | bytes 786432 | tf_op jit(solution)/shard_map/all_to_all | solution.py:459
  152.3 8.9 %all-to-all-done.3 = bf16[16,12,8,128]{3,2,1,0:T(8,128)(2,1)S(1)} async-done(((bf16[16,12,8,128]{3,2,1,0:T(8,128)(2,1)}), bf16[16,12,8,128]{3,2,1,0:T(8,128)(2,1)S(1)}, u32[]{:S(2)}, u32[]{:S(2)}) %all-to-all-start.3) | async-done | bytes 393248 | tf_op jit(solution)/shard_map/all_to_all | solution.py:459
  161.2 3.3 %update.1 = bf16[2,4,64,2048]{3,2,1,0:T(8,128)(2,1)} custom-call(bf16[1536,128]{1,0:T(8,128)(2,1)S(1)} %bitcast.12, bf16[2,192,1024]{2,1,0:T(8,128)(2,1)S(1)} %get-tuple-element.25.table, bf16[2,4,64,2048]{3,2,1,0:T(8,128)(2,1)S(1)} %bitcast.10, s32[2,4,64,1]{3,2,1,0:T(8,128)S(1)} %copy.7.onset), custom_call_target="tpu_custom_call" | custom-call | flops 402653184 | bytes 5242880 | tf_op jit(solution)/shard_map/update/pallas_call | solution.py:429
  (20 shorter events, 3.2 us)
Async XLA Ops:
  21.0 12.9 %collective-permute-start.3 = (bf16[12,16,1024]{2,1,0:T(8,128)(2,1)S(1)}, bf16[12,16,1024]{2,1,0:T(8,128)(2,1)S(1)}, u32[]{:S(2)}, u32[]{:S(2)}) collective-permute-start(bf16[12,16,1024]{2,1,0:T(8,128)(2,1)S(1)} %unfold.1.refs_0_), channel_id=1, source_target_pairs={{0,1},{1,0},{2,3},{3,2},{4,5},{5,4},{6,7},{7,6},{8,9},{9,8},{10,11... | collective-permute-start | bytes 1179656 | tf_op jit(solution)/shard_map/ppermute | solution.py:451
  24.6 14.3 %collective-permute-start = (bf16[12,16,1024]{2,1,0:T(8,128)(2,1)S(1)}, bf16[12,16,1024]{2,1,0:T(8,128)(2,1)S(1)}, u32[]{:S(2)}, u32[]{:S(2)}) collective-permute-start(bf16[12,16,1024]{2,1,0:T(8,128)(2,1)S(1)} %unfold.1.refs_0_), channel_id=1, source_target_pairs={{0,2},{1,3},{2,4},{3,5},{4,6},{5,7},{6,0},{7,1},{8,10},{9,11},{10,... | collective-permute-start | bytes 1179656 | tf_op jit(solution)/shard_map/ppermute | solution.py:451
  33.8 12.5 %collective-permute-start.5 = (bf16[12,16,1024]{2,1,0:T(8,128)(2,1)S(1)}, bf16[12,16,1024]{2,1,0:T(8,128)(2,1)S(1)}, u32[]{:S(2)}, u32[]{:S(2)}) collective-permute-start(bf16[12,16,1024]{2,1,0:T(8,128)(2,1)S(1)} %collective-permute-done.3.refs_4_), channel_id=1, source_target_pairs={{0,6},{1,7},{2,0},{3,1},{4,2},{5,3},{6,4},{7,5},{8,14},{9,15},{10,... | collective-permute-start | bytes 1179656 | tf_op jit(solution)/shard_map/ppermute | solution.py:451
  36.8 17.9 %collective-permute-start.1 = (bf16[12,16,1024]{2,1,0:T(8,128)(2,1)S(1)}, bf16[12,16,1024]{2,1,0:T(8,128)(2,1)S(1)}, u32[]{:S(2)}, u32[]{:S(2)}) collective-permute-start(bf16[12,16,1024]{2,1,0:T(8,128)(2,1)S(1)} %unfold.1.refs_0_), channel_id=1, source_target_pairs={{0,6},{1,7},{2,0},{3,1},{4,2},{5,3},{6,4},{7,5},{8,14},{9,15},{10,... | collective-permute-start | bytes 1179656 | tf_op jit(solution)/shard_map/ppermute | solution.py:451
  37.6 17.2 %collective-permute-start.4 = (bf16[12,16,1024]{2,1,0:T(8,128)(2,1)S(1)}, bf16[12,16,1024]{2,1,0:T(8,128)(2,1)S(1)}, u32[]{:S(2)}, u32[]{:S(2)}) collective-permute-start(bf16[12,16,1024]{2,1,0:T(8,128)(2,1)S(1)} %collective-permute-done.3.refs_4_), channel_id=1, source_target_pairs={{0,2},{1,3},{2,4},{3,5},{4,6},{5,7},{6,0},{7,1},{8,10},{9,11},{10,... | collective-permute-start | bytes 1179656 | tf_op jit(solution)/shard_map/ppermute | solution.py:451
  38.9 18.2 %collective-permute-start.2 = (bf16[12,16,1024]{2,1,0:T(8,128)(2,1)S(1)}, bf16[12,16,1024]{2,1,0:T(8,128)(2,1)S(1)}, u32[]{:S(2)}, u32[]{:S(2)}) collective-permute-start(bf16[12,16,1024]{2,1,0:T(8,128)(2,1)S(1)} %collective-permute-done.refs_1_), channel_id=1, source_target_pairs={{0,2},{1,3},{2,4},{3,5},{4,6},{5,7},{6,0},{7,1},{8,10},{9,11},{10,... | collective-permute-start | bytes 1179656 | tf_op jit(solution)/shard_map/ppermute | solution.py:451
  46.3 15.2 %collective-permute-start.6 = (bf16[12,16,1024]{2,1,0:T(8,128)(2,1)S(1)}, bf16[12,16,1024]{2,1,0:T(8,128)(2,1)S(1)}, u32[]{:S(2)}, u32[]{:S(2)}) collective-permute-start(bf16[12,16,1024]{2,1,0:T(8,128)(2,1)S(1)} %collective-permute-done.5.refs_6_), channel_id=1, source_target_pairs={{0,6},{1,7},{2,0},{3,1},{4,2},{5,3},{6,4},{7,5},{8,14},{9,15},{10,... | collective-permute-start | bytes 1179656 | tf_op jit(solution)/shard_map/ppermute | solution.py:451
  54.7 28.1 %copy-start.1 = (s32[4,256]{1,0:T(4,128)S(1)}, s32[4,256]{1,0:T(4,128)}, u32[]{:S(2)}) copy-start(s32[4,256]{1,0:T(4,128)} %onset.1) | copy-start | bytes 12292
  110.0 13.1 %collective-permute-start.10 = (bf16[12,16,1024]{2,1,0:T(8,128)(2,1)S(1)}, bf16[12,16,1024]{2,1,0:T(8,128)(2,1)S(1)}, u32[]{:S(2)}, u32[]{:S(2)}) collective-permute-start(bf16[12,16,1024]{2,1,0:T(8,128)(2,1)S(1)} %get-tuple-element.35), channel_id=1, source_target_pairs={{0,2},{1,3},{2,4},{3,5},{4,6},{5,7},{6,0},{7,1},{8,10},{9,11},{10,... | collective-permute-start | bytes 1179656 | tf_op jit(solution)/shard_map/ppermute | solution.py:451
  111.1 16.0 %collective-permute-start.7 = (bf16[12,16,1024]{2,1,0:T(8,128)(2,1)S(1)}, bf16[12,16,1024]{2,1,0:T(8,128)(2,1)S(1)}, u32[]{:S(2)}, u32[]{:S(2)}) collective-permute-start(bf16[12,16,1024]{2,1,0:T(8,128)(2,1)S(1)} %get-tuple-element.31), channel_id=1, source_target_pairs={{0,6},{1,7},{2,0},{3,1},{4,2},{5,3},{6,4},{7,5},{8,14},{9,15},{10,... | collective-permute-start | bytes 1179656 | tf_op jit(solution)/shard_map/ppermute | solution.py:451
  113.8 17.9 %collective-permute-start.12 = (bf16[12,16,1024]{2,1,0:T(8,128)(2,1)S(1)}, bf16[12,16,1024]{2,1,0:T(8,128)(2,1)S(1)}, u32[]{:S(2)}, u32[]{:S(2)}) collective-permute-start(bf16[12,16,1024]{2,1,0:T(8,128)(2,1)S(1)} %get-tuple-element.36), channel_id=1, source_target_pairs={{0,6},{1,7},{2,0},{3,1},{4,2},{5,3},{6,4},{7,5},{8,14},{9,15},{10,... | collective-permute-start | bytes 1179656 | tf_op jit(solution)/shard_map/ppermute | solution.py:451
  123.2 13.3 %collective-permute-start.11 = (bf16[12,16,1024]{2,1,0:T(8,128)(2,1)S(1)}, bf16[12,16,1024]{2,1,0:T(8,128)(2,1)S(1)}, u32[]{:S(2)}, u32[]{:S(2)}) collective-permute-start(bf16[12,16,1024]{2,1,0:T(8,128)(2,1)S(1)} %add_convert_fusion.1), channel_id=1, source_target_pairs={{0,2},{1,3},{2,4},{3,5},{4,6},{5,7},{6,0},{7,1},{8,10},{9,11},{10,... | collective-permute-start | bytes 1179656 | tf_op jit(solution)/shard_map/ppermute | solution.py:451
  126.3 25.8 %copy-start.2 = (s32[8,64]{1,0:T(8,128)S(1)}, s32[8,64]{1,0:T(8,128)}, u32[]{:S(2)}) copy-start(s32[8,64]{1,0:T(8,128)} %param.9) | copy-start | bytes 6148
  126.3 34.9 %copy-start = (bf16[8,64,2048]{2,1,0:T(8,128)(2,1)S(1)}, bf16[8,64,2048]{2,1,0:T(8,128)(2,1)}, u32[]{:S(2)}) copy-start(bf16[8,64,2048]{2,1,0:T(8,128)(2,1)} %param.6) | copy-start | bytes 6291460
  126.3 17.1 %collective-permute-start.9 = (bf16[12,16,1024]{2,1,0:T(8,128)(2,1)S(1)}, bf16[12,16,1024]{2,1,0:T(8,128)(2,1)S(1)}, u32[]{:S(2)}, u32[]{:S(2)}) collective-permute-start(bf16[12,16,1024]{2,1,0:T(8,128)(2,1)S(1)} %get-tuple-element.32), channel_id=1, source_target_pairs={{0,2},{1,3},{2,4},{3,5},{4,6},{5,7},{6,0},{7,1},{8,10},{9,11},{10,... | collective-permute-start | bytes 1179656 | tf_op jit(solution)/shard_map/ppermute | solution.py:451
  127.2 16.3 %collective-permute-start.8 = (bf16[12,16,1024]{2,1,0:T(8,128)(2,1)S(1)}, bf16[12,16,1024]{2,1,0:T(8,128)(2,1)S(1)}, u32[]{:S(2)}, u32[]{:S(2)}) collective-permute-start(bf16[12,16,1024]{2,1,0:T(8,128)(2,1)S(1)} %add_convert_fusion.2), channel_id=1, source_target_pairs={{0,6},{1,7},{2,0},{3,1},{4,2},{5,3},{6,4},{7,5},{8,14},{9,15},{10,... | collective-permute-start | bytes 1179656 | tf_op jit(solution)/shard_map/ppermute | solution.py:451
  136.7 9.8 %collective-permute-start.13 = (bf16[12,16,1024]{2,1,0:T(8,128)(2,1)S(1)}, bf16[12,16,1024]{2,1,0:T(8,128)(2,1)S(1)}, u32[]{:S(2)}, u32[]{:S(2)}) collective-permute-start(bf16[12,16,1024]{2,1,0:T(8,128)(2,1)S(1)} %add_convert_fusion), channel_id=1, source_target_pairs={{0,1},{1,0},{2,3},{3,2},{4,5},{5,4},{6,7},{7,6},{8,9},{9,8},{10,11... | collective-permute-start | bytes 1179656 | tf_op jit(solution)/shard_map/ppermute | solution.py:451
  148.4 12.8 %all-to-all-start.3 = ((bf16[16,12,8,128]{3,2,1,0:T(8,128)(2,1)}), bf16[16,12,8,128]{3,2,1,0:T(8,128)(2,1)S(1)}, u32[]{:S(2)}, u32[]{:S(2)}) async-start(bf16[16,12,8,128]{3,2,1,0:T(8,128)(2,1)} %fold.1), calls=%async_computation.3 | async-start | bytes 786432 | tf_op jit(solution)/shard_map/all_to_all | solution.py:459

commit v2 on v1

--- a/solution.py
+++ b/solution.py
@@ -41,15 +41,10 @@
 REMOTE = (FAR, ACROSS_UP, ACROSS_DOWN, ACROSS_FAR)
 
 
+LIMIT = 24 << 20
 VMEM_SPEC = pl.BlockSpec(memory_space=pltpu.VMEM)
 SMEM_SPEC = pl.BlockSpec(memory_space=pltpu.SMEM)
 HBM_SPEC = pl.BlockSpec(memory_space=pltpu.HBM)
-
-
-def params(limit=24):
-    return pltpu.CompilerParams(
-        dimension_semantics=("arbitrary",), vmem_limit_bytes=limit << 20
-    )
 
 
 def cost(flops, bytes_accessed):
@@ -101,39 +96,39 @@
     return (even + odd) * SCALE, (even - odd) * SCALE
 
 
-def spectrum_body(traces, table, out, wide):
-    step = pl.program_id(0)
-
-    @pl.when(step == 0)
-    def _():
-        write_table(table)
-
-    rows = traces[...].reshape(2 * RECV, NT).astype(F32)
-    for parity, bins in forward_bands(table, rows[:, :HT], rows[:, HT:]):
-        wide.at[parity][pl.ds(step, ROWS, stride=UP_POINTS), :] = bins
-
-    @pl.when(step == pl.num_programs(0) - 1)
-    def _():
-        for parity in range(BANDS):
-            for f in range(NFREQ):
-                out[f, parity] = wide[parity, f * PART : f * PART + PART].astype(BF16)
+def spectrum_body(traces, table, out, rows, wide, sems):
+    copies = [
+        pltpu.make_async_copy(traces.at[:, p], rows.at[p], sems.at[p]) for p in range(UP_POINTS)
+    ]
+    for copy in copies:
+        copy.start()
+    write_table(table)
+    for p, copy in enumerate(copies):
+        copy.wait()
+        early = rows[p, :, :, :HT].reshape(2 * RECV, HT).astype(F32)
+        late = rows[p, :, :, HT:].reshape(2 * RECV, HT).astype(F32)
+        for parity, bins in forward_bands(table, early, late):
+            wide.at[parity][pl.ds(p, ROWS, stride=UP_POINTS), :] = bins
+    for parity in range(BANDS):
+        for f in range(NFREQ):
+            out[f, parity] = wide[parity, f * PART : f * PART + PART].astype(BF16)
 
 
 def spectrum(traces):
     return pl.pallas_call(
         spectrum_body,
-        grid=(UP_POINTS,),
-        in_specs=[pl.BlockSpec((2, 1, RECV, NT), lambda i: (0, i, 0, 0))],
-        out_specs=[
-            pl.BlockSpec((BANDS, ROWS, HT), lambda i: (0, 0, 0)),
-            pl.BlockSpec((NFREQ, BANDS, PART, 128), lambda i: (0, 0, 0, 0)),
-        ],
+        in_specs=[HBM_SPEC],
+        out_specs=[VMEM_SPEC] * 2,
         out_shape=[
             jax.ShapeDtypeStruct((BANDS, ROWS, HT), BF16),
             jax.ShapeDtypeStruct((NFREQ, BANDS, PART, 128), BF16),
         ],
-        scratch_shapes=[pltpu.VMEM((BANDS, WIDE, 128), F32)],
-        compiler_params=params(),
+        scratch_shapes=[
+            pltpu.VMEM((UP_POINTS, 2, RECV, NT), BF16),
+            pltpu.VMEM((BANDS, WIDE, 128), F32),
+            pltpu.SemaphoreType.DMA((UP_POINTS,)),
+        ],
+        compiler_params=pltpu.CompilerParams(vmem_limit_bytes=LIMIT),
         cost_estimate=cost(POINTS * RECV * NT * 2 * ROWS, 4 << 20),
         name="spectrum",
     )(traces)
@@ -209,9 +204,9 @@
         for parity in range(BANDS):
             j = parity * J2 + j2
             at = BANDS * j2 + parity
-            field = jnp.concatenate([b[j] for b in blocks], axis=0)
-            by_real = lax.dot_general(field, kern[0, at], NT_DIMS, preferred_element_type=F32)
-            by_imag = lax.dot_general(field, kern[1, at], NT_DIMS, preferred_element_type=F32)
+            field = jnp.concatenate([b[j] for b in blocks], axis=0).T
+            by_real = jnp.dot(kern[0, at], field, preferred_element_type=F32).T
+            by_imag = jnp.dot(kern[1, at], field, preferred_element_type=F32).T
             waves = (by_real + swapped(by_imag, 1.0)).astype(BF16).reshape(NSRC, 2, 8, SOURCES)
             for rel in range(NSRC):
                 for half in range(2):
@@ -336,6 +331,7 @@
     )(*terms)
 
 
+PER = 2
 LANES = [slice(half * 128, half * 128 + 128) for half in range(SOURCES // 128)]
 
 
@@ -346,99 +342,97 @@
             yield parity, slice(f * PART, f * PART + PART), slice(start, start + PART)
 
 
-def truncate_body(waves, table, onset, up, back, wide_in, wide_out):
-    step = pl.program_id(0)
-
-    @pl.when(step == 0)
-    def _():
-        for parity, inner, outer in parts():
-            for half, lanes in enumerate(LANES):
-                wide_in[parity, half, inner] = waves[outer, lanes].astype(F32)
-
-    every = pl.ds(step, ROWS, stride=UP_POINTS)
-    bands = [
-        jnp.concatenate(
-            [wide_in.at[parity, half][every, :] for half in range(len(LANES))], axis=1
-        ).astype(BF16)
-        for parity in range(BANDS)
-    ]
-    limit = onset[pl.ds(step, 1), :].astype(F32)
-    limit = jnp.broadcast_to(limit, (128, SOURCES)).T[:, :1].astype(jnp.int32)
-    sample = lax.broadcasted_iota(jnp.int32, (SOURCES, HT), 1)
-    kept = []
-    for half, signal in enumerate(inverse_bands(table, bands)):
-        kept.append(jnp.where(sample < limit - half * HT, signal, 0.0).astype(BF16))
-        up[:, half * HT : half * HT + HT] = kept[-1]
-    for parity, bins in forward_bands(table, kept[0].astype(F32), kept[1].astype(F32)):
+def truncate_body(waves, table, onset, up, back, wide_in, wide_out, rows, sems):
+    for parity, inner, outer in parts():
         for half, lanes in enumerate(LANES):
-            wide_out.at[parity, half][every, :] = bins[:, lanes]
-
-    @pl.when(step == pl.num_programs(0) - 1)
-    def _():
-        for parity, inner, outer in parts():
-            for half, lanes in enumerate(LANES):
-                back[outer, lanes] = wide_out[parity, half, inner].astype(BF16)
+            wide_in[parity, half, inner] = waves[outer, lanes].astype(F32)
+    sample = lax.broadcasted_iota(jnp.int32, (PER * SOURCES, HT), 1)
+    copies = []
+    for group in range(UP_POINTS // PER):
+        points = [PER * group + index for index in range(PER)]
+        every = [pl.ds(point, ROWS, stride=UP_POINTS) for point in points]
+        bands = [
+            jnp.concatenate(
+                [wide_in.at[parity, half][e, :] for e in every for half in range(len(LANES))], axis=1
+            ).astype(BF16)
+            for parity in range(BANDS)
+        ]
+        limit = [
+            jnp.broadcast_to(onset[p : p + 1, :].astype(F32), (128, SOURCES)).T[:, :1] for p in points
+        ]
+        limit = jnp.concatenate(limit, axis=0).astype(jnp.int32)
+        kept = []
+        for half, signal in enumerate(inverse_bands(table, bands)):
+            kept.append(jnp.where(sample < limit - half * HT, signal, 0.0).astype(BF16))
+            rows[group, :, half * HT : half * HT + HT] = kept[-1]
+        span = pl.ds(group * PER * SOURCES, PER * SOURCES)
+        copies.append(pltpu.make_async_copy(rows.at[group], up.at[span], sems.at[group]))
+        copies[-1].start()
+        for parity, bins in forward_bands(table, kept[0].astype(F32), kept[1].astype(F32)):
+            for index, e in enumerate(every):
+                for half in range(len(LANES)):
+                    start = index * SOURCES + half * 128
+                    wide_out.at[parity, half][e, :] = bins[:, start : start + 128]
+    for parity, inner, outer in parts():
+        for half, lanes in enumerate(LANES):
+            back[outer, lanes] = wide_out[parity, half, inner].astype(BF16)
+    for copy in copies:
+        copy.wait()
 
 
 def truncate(waves, table, onset):
-    rows = waves.shape[0]
+    groups = UP_POINTS // PER
     return pl.pallas_call(
         truncate_body,
-        grid=(UP_POINTS,),
-        in_specs=[
-            pl.BlockSpec((rows, SOURCES), lambda i: (0, 0)),
-            pl.BlockSpec((BANDS, ROWS, HT), lambda i: (0, 0, 0)),
-            pl.BlockSpec((UP_POINTS, SOURCES), lambda i: (0, 0)),
+        in_specs=[VMEM_SPEC] * 3,
+        out_specs=[pl.BlockSpec(memory_space=pl.ANY), VMEM_SPEC],
+        out_shape=[
+            pltpu.HBM((UP_POINTS * SOURCES, NT), BF16),
+            jax.ShapeDtypeStruct(waves.shape, BF16),
         ],
-        out_specs=[
-            pl.BlockSpec((SOURCES, NT), lambda i: (i, 0)),
-            pl.BlockSpec((rows, SOURCES), lambda i: (0, 0)),
+        scratch_shapes=[pltpu.VMEM((BANDS, len(LANES), WIDE, 128), F32)] * 2
+        + [
+            pltpu.VMEM((groups, PER * SOURCES, NT), BF16),
+            pltpu.SemaphoreType.DMA((groups,)),
         ],
-        out_shape=[
-            jax.ShapeDtypeStruct((UP_POINTS * SOURCES, NT), BF16),
-            jax.ShapeDtypeStruct((rows, SOURCES), BF16),
-        ],
-        scratch_shapes=[pltpu.VMEM((BANDS, len(LANES), WIDE, 128), F32)] * 2,
-        compiler_params=params(),
+        compiler_params=pltpu.CompilerParams(vmem_limit_bytes=40 << 20),
         cost_estimate=cost(2 * UP_POINTS * SOURCES * NT * 2 * ROWS, 8 << 20),
         name="truncate",
     )(waves, table, onset)
 
 
-def update_body(bins, table, direct, onset, out, wide):
-    step = pl.program_id(0)
-
-    @pl.when(step == 0)
-    def _():
-        for parity, inner, outer in parts():
-            wide[parity, inner] = bins[outer, :].astype(F32)
-
-    every = pl.ds(step, ROWS, stride=UP_POINTS)
-    bands = [wide.at[parity][every, :].astype(BF16) for parity in range(BANDS)]
-    limit = onset[...].reshape(2 * RECV, 1)
+def update_body(bins, table, direct, onset, out, wide, rows, sems):
+    for parity, inner, outer in parts():
+        wide[parity, inner] = bins[outer, :].astype(F32)
     sample = lax.broadcasted_iota(jnp.int32, (2 * RECV, HT), 1)
-    for half, trace in enumerate(inverse_bands(table, bands)):
-        span = slice(half * HT, half * HT + HT)
-        cut = jnp.where(sample < limit - half * HT, trace, 0.0)
-        before = direct[:, 0, :, span].reshape(2 * RECV, HT).astype(F32)
-        out[:, 0, :, span] = (before - cut).astype(BF16).reshape(2, RECV, HT)
+    copies = []
+    for p in range(UP_POINTS):
+        every = pl.ds(p, ROWS, stride=UP_POINTS)
+        bands = [wide.at[parity][every, :].astype(BF16) for parity in range(BANDS)]
+        limit = onset[:, p].reshape(2 * RECV, 1)
+        for half, trace in enumerate(inverse_bands(table, bands)):
+            span = slice(half * HT, half * HT + HT)
+            cut = jnp.where(sample < limit - half * HT, trace, 0.0)
+            before = direct[:, p, :, span].reshape(2 * RECV, HT).astype(F32)
+            rows[p, :, :, span] = (before - cut).astype(BF16).reshape(2, RECV, HT)
+        copies.append(pltpu.make_async_copy(rows.at[p], out.at[:, p], sems.at[p]))
+        copies[-1].start()
+    for copy in copies:
+        copy.wait()
 
 
 def update(bins, table, direct, onset):
-    rows = bins.shape[0]
     return pl.pallas_call(
         update_body,
-        grid=(UP_POINTS,),
-        in_specs=[
-            pl.BlockSpec((rows, 2 * RECV), lambda i: (0, 0)),
-            pl.BlockSpec((BANDS, ROWS, HT), lambda i: (0, 0, 0)),
-            pl.BlockSpec((2, 1, RECV, NT), lambda i: (0, i, 0, 0)),
-            pl.BlockSpec((2, 1, RECV, 1), lambda i: (0, i, 0, 0)),
+        in_specs=[VMEM_SPEC] * 4,
+        out_specs=pl.BlockSpec(memory_space=pl.ANY),
+        out_shape=pltpu.HBM((2, UP_POINTS, RECV, NT), BF16),
+        scratch_shapes=[
+            pltpu.VMEM((BANDS, WIDE, 2 * RECV), F32),
+            pltpu.VMEM((UP_POINTS, 2, RECV, NT), BF16),
+            pltpu.SemaphoreType.DMA((UP_POINTS,)),
         ],
-        out_specs=pl.BlockSpec((2, 1, RECV, NT), lambda i: (0, i, 0, 0)),
-        out_shape=jax.ShapeDtypeStruct((2, UP_POINTS, RECV, NT), BF16),
-        scratch_shapes=[pltpu.VMEM((BANDS, WIDE, 2 * RECV), F32)],
-        compiler_params=params(),
+        compiler_params=pltpu.CompilerParams(vmem_limit_bytes=LIMIT),
         cost_estimate=cost(POINTS * RECV * NT * 2 * ROWS, 5 << 20),
         name="update",
     )(bins, table, direct, onset)

time: 166 us -> 162 us (0.976)
  Pallas kernels: 34.7 us -> 30.5 us
    pallas_call x3, Pallas kernels: 14.1 us -> 10.1 us  [the longest x1 4.82 us: truncate(): pl.pallas_call(truncate_body, in_specs=[VMEM_SPEC] * 3, out_specs=[pl.Blo...]
where the time goes in v2:
time: 162 us; the launch traced here: 161 us
  waiting for transfers between devices  51.4 us (32%)
  blocking collectives  46.8 us (29%)
  Pallas kernels  30.5 us (19%)
  starting transfers between devices  30.5 us (19%)
    all_to_all x3, blocking collectives, exchange(): lax.all_to_all(value, 'freq', split_axis=0, concat_axis=0, tiled=True)  46.8 us
    ppermute x14, waiting for transfers between devices, shift(): return lax.ppermute(value, 'src', pairs)  42.5 us
    ppermute x14, starting transfers between devices, shift(): return lax.ppermute(value, 'src', pairs)  26.7 us
    all_to_all x1, waiting for transfers between devices, exchange(): lax.all_to_all(value, 'freq', split_axis=0, concat_axis=0, tiled=True)  8.91 us
    pallas_call x1, Pallas kernels, adjoint_remote(): pl.pallas_call(adjoint_remote_body, in_specs=[SMEM_SPEC, VMEM_SPEC, HBM_S...  5.11 us
    pallas_call x1, Pallas kernels, forward(): pl.pallas_call(forward_body, in_specs=[SMEM_SPEC] + [VMEM_SPEC] * (NSRC +...  4.9 us
    pallas_call x1, Pallas kernels, truncate(): pl.pallas_call(truncate_body, in_specs=[VMEM_SPEC] * 3, out_specs=[pl.Blo...  4.82 us
    pallas_call x1, Pallas kernels, hold(): pl.pallas_call(hold_body, in_specs=[HBM_SPEC], out_specs=pl.BlockSpec(mem...  4.62 us
  transfers between devices with their start and end apart: 15, of which 11 were waited for; matrix products, arithmetic and copies ran while one was open for 0% of the time, Pallas kernels for 5%

profile of v2, /device:TPU:0, one launch (start us, length us, event | category | flops | bytes accessed | tf_op | source)
XLA Modules:
  0.0 160.7 jit_solution(2038165582877131836)
XLA Ops:
  0.6 2.9 %spectrum.1 = (bf16[2,192,1024]{2,1,0:T(8,128)(2,1)S(1)}, bf16[16,2,48,128]{3,2,1,0:T(8,128)(2,1)S(1)}) custom-call(bf16[2,4,64,2048]{3,2,1,0:T(8,128)(2,1)} %bitcast.15), custom_call_target="tpu_custom_call" | custom-call | flops 402653184 | bytes 4194304 | tf_op jit(solution)/shard_map/spectrum/pallas_call | solution.py:118
  3.5 14.8 %all_to_all.20 = bf16[16,2,48,128]{3,2,1,0:T(8,128)(2,1)S(1)} all-to-all(bf16[16,2,48,128]{3,2,1,0:T(8,128)(2,1)S(1)} %get-tuple-element.22), channel_id=1, replica_groups=mesh['freq'=16,'src'=8] {'freq'}, dimensions={0} | all-to-all | bytes 786432 | tf_op jit(solution)/shard_map/all_to_all | solution.py:453
  19.2 3.7 %collective-permute-start.3 = (bf16[12,16,1024]{2,1,0:T(8,128)(2,1)S(1)}, bf16[12,16,1024]{2,1,0:T(8,128)(2,1)S(1)}, u32[]{:S(2)}, u32[]{:S(2)}) collective-permute-start(bf16[12,16,1024]{2,1,0:T(8,128)(2,1)S(1)} %unfold.1.refs_0_), channel_id=1, source_target_pairs={{0,1},{1,0},{2,3},{3,2},{4,5},{5,4},{6,7},{7,6},{8,9},{9,8},{10,11... | collective-permute-start | bytes 1179656 | tf_op jit(solution)/shard_map/ppermute | solution.py:445
  22.9 1.6 collective-permute-start
  24.5 7.6 %collective-permute-done.3.refs_4_ = bf16[12,16,1024]{2,1,0:T(8,128)(2,1)S(1)} collective-permute-done((bf16[12,16,1024]{2,1,0:T(8,128)(2,1)S(1)}, bf16[12,16,1024]{2,1,0:T(8,128)(2,1)S(1)}, u32[]{:S(2)}, u32[]{:S(2)}) %collective-permute-start.3) | collective-permute-done | bytes 393248 | tf_op jit(solution)/shard_map/ppermute | solution.py:445
  32.1 3.0 %collective-permute-start.5 = (bf16[12,16,1024]{2,1,0:T(8,128)(2,1)S(1)}, bf16[12,16,1024]{2,1,0:T(8,128)(2,1)S(1)}, u32[]{:S(2)}, u32[]{:S(2)}) collective-permute-start(bf16[12,16,1024]{2,1,0:T(8,128)(2,1)S(1)} %collective-permute-done.3.refs_4_), channel_id=1, source_target_pairs={{0,6},{1,7},{2,0},{3,1},{4,2},{5,3},{6,4},{7,5},{8,14},{9,15},{10,... | collective-permute-start | bytes 1179656 | tf_op jit(solution)/shard_map/ppermute | solution.py:445
  35.9 1.3 collective-permute-start.4
  37.2 7.5 %collective-permute-done.5.refs_6_ = bf16[12,16,1024]{2,1,0:T(8,128)(2,1)S(1)} collective-permute-done((bf16[12,16,1024]{2,1,0:T(8,128)(2,1)S(1)}, bf16[12,16,1024]{2,1,0:T(8,128)(2,1)S(1)}, u32[]{:S(2)}, u32[]{:S(2)}) %collective-permute-start.5) | collective-permute-done | bytes 393248 | tf_op jit(solution)/shard_map/ppermute | solution.py:445
  44.6 3.7 %collective-permute-start.6 = (bf16[12,16,1024]{2,1,0:T(8,128)(2,1)S(1)}, bf16[12,16,1024]{2,1,0:T(8,128)(2,1)S(1)}, u32[]{:S(2)}, u32[]{:S(2)}) collective-permute-start(bf16[12,16,1024]{2,1,0:T(8,128)(2,1)S(1)} %collective-permute-done.5.refs_6_), channel_id=1, source_target_pairs={{0,6},{1,7},{2,0},{3,1},{4,2},{5,3},{6,4},{7,5},{8,14},{9,15},{10,... | collective-permute-start | bytes 1179656 | tf_op jit(solution)/shard_map/ppermute | solution.py:445
  48.3 4.6 %hold.1.refs_8_ = bf16[2,12,256,1024]{3,2,1,0:T(8,128)(2,1)S(1)} custom-call(bf16[2,12,256,1024]{3,2,1,0:T(8,128)(2,1)} %kern.2), custom_call_target="tpu_custom_call" | custom-call | bytes 13631488 | tf_op jit(solution)/shard_map/hold/pallas_call | solution.py:187
  53.0 2.3 %collective-permute-done.2.refs_3_ = bf16[12,16,1024]{2,1,0:T(8,128)(2,1)S(1)} collective-permute-done((bf16[12,16,1024]{2,1,0:T(8,128)(2,1)S(1)}, bf16[12,16,1024]{2,1,0:T(8,128)(2,1)S(1)}, u32[]{:S(2)}, u32[]{:S(2)}) %collective-permute-start.2) | collective-permute-done | bytes 393248 | tf_op jit(solution)/shard_map/ppermute | solution.py:445
  55.3 4.6 %collective-permute-done.6.refs_7_ = bf16[12,16,1024]{2,1,0:T(8,128)(2,1)S(1)} collective-permute-done((bf16[12,16,1024]{2,1,0:T(8,128)(2,1)S(1)}, bf16[12,16,1024]{2,1,0:T(8,128)(2,1)S(1)}, u32[]{:S(2)}, u32[]{:S(2)}) %collective-permute-start.6) | collective-permute-done | bytes 393248 | tf_op jit(solution)/shard_map/ppermute | solution.py:445
  59.9 4.9 %forward.1 = bf16[16,12,8,256]{3,2,1,0:T(8,128)(2,1)S(1)} custom-call(s32[1]{0:T(128)} %bitcast.1.me, bf16[12,16,1024]{2,1,0:T(8,128)(2,1)S(1)} %unfold.1.refs_0_, bf16[12,16,1024]{2,1,0:T(8,128)(2,1)S(1)} %collective-permute-done.refs_1_, bf16[12,16,1024]{2,1,0:T(8,128)(2,1)S(1)} %collective-permute-done.1.refs_2_, ...), custom_call_target="tpu_custom_call" | custom-call | flops 1610612736 | bytes 4194304 | tf_op jit(solution)/shard_map/forward/pallas_call | solution.py:220
  64.8 16.1 %all_to_all.21 = bf16[16,12,8,256]{3,2,1,0:T(8,128)(2,1)S(1)} all-to-all(bf16[16,12,8,256]{3,2,1,0:T(8,128)(2,1)S(1)} %forward.1), channel_id=1, replica_groups=mesh['freq'=16,'src'=8] {'freq'}, dimensions={0} | all-to-all | bytes 1572864 | tf_op jit(solution)/shard_map/all_to_all | solution.py:453
  80.9 4.8 %truncate.1 = (bf16[1024,2048]{1,0:T(8,128)(2,1)}, bf16[1536,256]{1,0:T(8,128)(2,1)S(1)}) custom-call(bf16[1536,256]{1,0:T(8,128)(2,1)S(1)} %bitcast.13, bf16[2,192,1024]{2,1,0:T(8,128)(2,1)S(1)} %get-tuple-element.25.table, s32[4,256]{1,0:T(4,128)S(1)} %copy-done.1), custom_call_target="tpu_custom_call" | custom-call | flops 1610612736 | bytes 8388608 | tf_op jit(solution)/shard_map/truncate/pallas_call | solution.py:385
  85.7 15.9 %all_to_all.22.field_ref = bf16[16,12,8,256]{3,2,1,0:T(8,128)(2,1)S(1)} all-to-all(bf16[16,12,8,256]{3,2,1,0:T(8,128)(2,1)S(1)} %bitcast.14), channel_id=1, replica_groups=mesh['freq'=16,'src'=8] {'freq'}, dimensions={0} | all-to-all | bytes 1572864 | tf_op jit(solution)/shard_map/all_to_all | solution.py:453
  101.6 5.1 %adjoint_remote.1 = (bf16[12,16,1024]{2,1,0:T(8,128)(2,1)S(1)}, bf16[12,16,1024]{2,1,0:T(8,128)(2,1)S(1)}, bf16[12,16,1024]{2,1,0:T(8,128)(2,1)S(1)}, bf16[12,16...) custom-call(s32[1]{0:T(128)} %bitcast.1.me, bf16[16,12,8,256]{3,2,1,0:T(8,128)(2,1)S(1)} %all_to_all.22.field_ref, ...), custom_call_target="tpu_custom_call" | custom-call | flops 805306368 | bytes 14680064 | tf_op jit(solution)/shard_map/adjoint_remote/pallas_call | solution.py:270
  106.7 1.1 collective-permute-start.10
  107.9 2.7 %collective-permute-start.7 = (bf16[12,16,1024]{2,1,0:T(8,128)(2,1)S(1)}, bf16[12,16,1024]{2,1,0:T(8,128)(2,1)S(1)}, u32[]{:S(2)}, u32[]{:S(2)}) collective-permute-start(bf16[12,16,1024]{2,1,0:T(8,128)(2,1)S(1)} %get-tuple-element.31), channel_id=1, source_target_pairs={{0,6},{1,7},{2,0},{3,1},{4,2},{5,3},{6,4},{7,5},{8,14},{9,15},{10,... | collective-permute-start | bytes 1179656 | tf_op jit(solution)/shard_map/ppermute | solution.py:445
  110.6 1.9 %collective-permute-start.12 = (bf16[12,16,1024]{2,1,0:T(8,128)(2,1)S(1)}, bf16[12,16,1024]{2,1,0:T(8,128)(2,1)S(1)}, u32[]{:S(2)}, u32[]{:S(2)}) collective-permute-start(bf16[12,16,1024]{2,1,0:T(8,128)(2,1)S(1)} %get-tuple-element.36), channel_id=1, source_target_pairs={{0,6},{1,7},{2,0},{3,1},{4,2},{5,3},{6,4},{7,5},{8,14},{9,15},{10,... | collective-permute-start | bytes 1179656 | tf_op jit(solution)/shard_map/ppermute | solution.py:445
  112.5 7.3 %collective-permute-done.10 = bf16[12,16,1024]{2,1,0:T(8,128)(2,1)S(1)} collective-permute-done((bf16[12,16,1024]{2,1,0:T(8,128)(2,1)S(1)}, bf16[12,16,1024]{2,1,0:T(8,128)(2,1)S(1)}, u32[]{:S(2)}, u32[]{:S(2)}) %collective-permute-start.10) | collective-permute-done | bytes 393248 | tf_op jit(solution)/shard_map/ppermute | solution.py:445
  120.3 3.0 %adjoint_near.1 = (bf16[12,16,1024]{2,1,0:T(8,128)(2,1)S(1)}, bf16[12,16,1024]{2,1,0:T(8,128)(2,1)S(1)}, bf16[12,16,1024]{2,1,0:T(8,128)(2,1)S(1)}, bf16[12,16,1024]{2,1,0:T(8,128)(2,1)S(1)}) custom-call(s32[1]{0:T(128)} %bitcast.1.me, bf16[16,12,8,256]{3,2,1,0:T(8,128)(2,1)S(1)} %all_to_all.22.field_ref, bf16[2,12,256,1024]{3,2,1,0:T(8,128)(2,1)S(1)} %get-tuple-element.28.held), custom_call_target="tpu_custom_call" | custom-call | flops 805306368 | bytes 2097152 | tf_op jit(solution)/shard_map/adjoint_near/pallas_call | solution.py:295
  124.1 2.7 %collective-permute-start.8 = (bf16[12,16,1024]{2,1,0:T(8,128)(2,1)S(1)}, bf16[12,16,1024]{2,1,0:T(8,128)(2,1)S(1)}, u32[]{:S(2)}, u32[]{:S(2)}) collective-permute-start(bf16[12,16,1024]{2,1,0:T(8,128)(2,1)S(1)} %add_convert_fusion.2), channel_id=1, source_target_pairs={{0,6},{1,7},{2,0},{3,1},{4,2},{5,3},{6,4},{7,5},{8,14},{9,15},{10,... | collective-permute-start | bytes 1179656 | tf_op jit(solution)/shard_map/ppermute | solution.py:445
  126.8 1.7 %collective-permute-done.12 = bf16[12,16,1024]{2,1,0:T(8,128)(2,1)S(1)} collective-permute-done((bf16[12,16,1024]{2,1,0:T(8,128)(2,1)S(1)}, bf16[12,16,1024]{2,1,0:T(8,128)(2,1)S(1)}, u32[]{:S(2)}, u32[]{:S(2)}) %collective-permute-start.12) | collective-permute-done | bytes 393248 | tf_op jit(solution)/shard_map/ppermute | solution.py:445
  128.5 4.9 %collective-permute-done.11 = bf16[12,16,1024]{2,1,0:T(8,128)(2,1)S(1)} collective-permute-done((bf16[12,16,1024]{2,1,0:T(8,128)(2,1)S(1)}, bf16[12,16,1024]{2,1,0:T(8,128)(2,1)S(1)}, u32[]{:S(2)}, u32[]{:S(2)}) %collective-permute-start.11) | collective-permute-done | bytes 393248 | tf_op jit(solution)/shard_map/ppermute | solution.py:445
  133.7 3.3 %collective-permute-start.13 = (bf16[12,16,1024]{2,1,0:T(8,128)(2,1)S(1)}, bf16[12,16,1024]{2,1,0:T(8,128)(2,1)S(1)}, u32[]{:S(2)}, u32[]{:S(2)}) collective-permute-start(bf16[12,16,1024]{2,1,0:T(8,128)(2,1)S(1)} %add_convert_fusion), channel_id=1, source_target_pairs={{0,1},{1,0},{2,3},{3,2},{4,5},{5,4},{6,7},{7,6},{8,9},{9,8},{10,11... | collective-permute-start | bytes 1179656 | tf_op jit(solution)/shard_map/ppermute | solution.py:445
  137.0 3.4 %collective-permute-done.9.refs_2_ = bf16[12,16,1024]{2,1,0:T(8,128)(2,1)S(1)} collective-permute-done((bf16[12,16,1024]{2,1,0:T(8,128)(2,1)S(1)}, bf16[12,16,1024]{2,1,0:T(8,128)(2,1)S(1)}, u32[]{:S(2)}, u32[]{:S(2)}) %collective-permute-start.9) | collective-permute-done | bytes 393248 | tf_op jit(solution)/shard_map/ppermute | solution.py:445
  140.4 3.0 %collective-permute-done.13.refs_3_ = bf16[12,16,1024]{2,1,0:T(8,128)(2,1)S(1)} collective-permute-done((bf16[12,16,1024]{2,1,0:T(8,128)(2,1)S(1)}, bf16[12,16,1024]{2,1,0:T(8,128)(2,1)S(1)}, u32[]{:S(2)}, u32[]{:S(2)}) %collective-permute-start.13) | collective-permute-done | bytes 393248 | tf_op jit(solution)/shard_map/ppermute | solution.py:445
  143.5 1.8 %fold.1 = bf16[16,12,8,128]{3,2,1,0:T(8,128)(2,1)} custom-call(bf16[12,16,1024]{2,1,0:T(8,128)(2,1)S(1)} %get-tuple-element.29.refs_0_, bf16[12,16,1024]{2,1,0:T(8,128)(2,1)S(1)} %collective-permute-done.8.refs_1_, bf16[12,16,1024]{2,1,0:T(8,128)(2,1)S(1)} %collective-permute-done.9.refs_2_, bf16[12,16,1024]{2,1,0:T(8,128)(2,1)S(1)} %collective-permute-done.13.refs_3_), custom_call_target="tpu_custom_call" | custom-call | bytes 2097152 | tf_op jit(solution)/shard_map/fold/pallas_call | solution.py:323
  145.3 3.7 %all-to-all-start.3 = ((bf16[16,12,8,128]{3,2,1,0:T(8,128)(2,1)}), bf16[16,12,8,128]{3,2,1,0:T(8,128)(2,1)S(1)}, u32[]{:S(2)}, u32[]{:S(2)}) async-start(bf16[16,12,8,128]{3,2,1,0:T(8,128)(2,1)} %fold.1), calls=%async_computation.3 | async-start | bytes 786432 | tf_op jit(solution)/shard_map/all_to_all | solution.py:453
  149.2 8.9 %all-to-all-done.3 = bf16[16,12,8,128]{3,2,1,0:T(8,128)(2,1)S(1)} async-done(((bf16[16,12,8,128]{3,2,1,0:T(8,128)(2,1)}), bf16[16,12,8,128]{3,2,1,0:T(8,128)(2,1)S(1)}, u32[]{:S(2)}, u32[]{:S(2)}) %all-to-all-start.3) | async-done | bytes 393248 | tf_op jit(solution)/shard_map/all_to_all | solution.py:453
  158.1 2.4 %update.1 = bf16[2,4,64,2048]{3,2,1,0:T(8,128)(2,1)} custom-call(bf16[1536,128]{1,0:T(8,128)(2,1)S(1)} %bitcast.12, bf16[2,192,1024]{2,1,0:T(8,128)(2,1)S(1)} %get-tuple-element.25.table, bf16[2,4,64,2048]{3,2,1,0:T(8,128)(2,1)S(1)} %bitcast.10, s32[2,4,64,1]{3,2,1,0:T(8,128)S(1)} %copy.7.onset), custom_call_target="tpu_custom_call" | custom-call | flops 402653184 | bytes 5242880 | tf_op jit(solution)/shard_map/update/pallas_call | solution.py:425
  (20 shorter events, 3.4 us)
Async XLA Ops:
  19.2 12.9 %collective-permute-start.3 = (bf16[12,16,1024]{2,1,0:T(8,128)(2,1)S(1)}, bf16[12,16,1024]{2,1,0:T(8,128)(2,1)S(1)}, u32[]{:S(2)}, u32[]{:S(2)}) collective-permute-start(bf16[12,16,1024]{2,1,0:T(8,128)(2,1)S(1)} %unfold.1.refs_0_), channel_id=1, source_target_pairs={{0,1},{1,0},{2,3},{3,2},{4,5},{5,4},{6,7},{7,6},{8,9},{9,8},{10,11... | collective-permute-start | bytes 1179656 | tf_op jit(solution)/shard_map/ppermute | solution.py:445
  22.9 14.2 %collective-permute-start = (bf16[12,16,1024]{2,1,0:T(8,128)(2,1)S(1)}, bf16[12,16,1024]{2,1,0:T(8,128)(2,1)S(1)}, u32[]{:S(2)}, u32[]{:S(2)}) collective-permute-start(bf16[12,16,1024]{2,1,0:T(8,128)(2,1)S(1)} %unfold.1.refs_0_), channel_id=1, source_target_pairs={{0,2},{1,3},{2,4},{3,5},{4,6},{5,7},{6,0},{7,1},{8,10},{9,11},{10,... | collective-permute-start | bytes 1179656 | tf_op jit(solution)/shard_map/ppermute | solution.py:445
  32.1 12.5 %collective-permute-start.5 = (bf16[12,16,1024]{2,1,0:T(8,128)(2,1)S(1)}, bf16[12,16,1024]{2,1,0:T(8,128)(2,1)S(1)}, u32[]{:S(2)}, u32[]{:S(2)}) collective-permute-start(bf16[12,16,1024]{2,1,0:T(8,128)(2,1)S(1)} %collective-permute-done.3.refs_4_), channel_id=1, source_target_pairs={{0,6},{1,7},{2,0},{3,1},{4,2},{5,3},{6,4},{7,5},{8,14},{9,15},{10,... | collective-permute-start | bytes 1179656 | tf_op jit(solution)/shard_map/ppermute | solution.py:445
  35.1 17.9 %collective-permute-start.1 = (bf16[12,16,1024]{2,1,0:T(8,128)(2,1)S(1)}, bf16[12,16,1024]{2,1,0:T(8,128)(2,1)S(1)}, u32[]{:S(2)}, u32[]{:S(2)}) collective-permute-start(bf16[12,16,1024]{2,1,0:T(8,128)(2,1)S(1)} %unfold.1.refs_0_), channel_id=1, source_target_pairs={{0,6},{1,7},{2,0},{3,1},{4,2},{5,3},{6,4},{7,5},{8,14},{9,15},{10,... | collective-permute-start | bytes 1179656 | tf_op jit(solution)/shard_map/ppermute | solution.py:445
  35.9 17.2 %collective-permute-start.4 = (bf16[12,16,1024]{2,1,0:T(8,128)(2,1)S(1)}, bf16[12,16,1024]{2,1,0:T(8,128)(2,1)S(1)}, u32[]{:S(2)}, u32[]{:S(2)}) collective-permute-start(bf16[12,16,1024]{2,1,0:T(8,128)(2,1)S(1)} %collective-permute-done.3.refs_4_), channel_id=1, source_target_pairs={{0,2},{1,3},{2,4},{3,5},{4,6},{5,7},{6,0},{7,1},{8,10},{9,11},{10,... | collective-permute-start | bytes 1179656 | tf_op jit(solution)/shard_map/ppermute | solution.py:445
  37.1 18.2 %collective-permute-start.2 = (bf16[12,16,1024]{2,1,0:T(8,128)(2,1)S(1)}, bf16[12,16,1024]{2,1,0:T(8,128)(2,1)S(1)}, u32[]{:S(2)}, u32[]{:S(2)}) collective-permute-start(bf16[12,16,1024]{2,1,0:T(8,128)(2,1)S(1)} %collective-permute-done.refs_1_), channel_id=1, source_target_pairs={{0,2},{1,3},{2,4},{3,5},{4,6},{5,7},{6,0},{7,1},{8,10},{9,11},{10,... | collective-permute-start | bytes 1179656 | tf_op jit(solution)/shard_map/ppermute | solution.py:445
  44.6 15.2 %collective-permute-start.6 = (bf16[12,16,1024]{2,1,0:T(8,128)(2,1)S(1)}, bf16[12,16,1024]{2,1,0:T(8,128)(2,1)S(1)}, u32[]{:S(2)}, u32[]{:S(2)}) collective-permute-start(bf16[12,16,1024]{2,1,0:T(8,128)(2,1)S(1)} %collective-permute-done.5.refs_6_), channel_id=1, source_target_pairs={{0,6},{1,7},{2,0},{3,1},{4,2},{5,3},{6,4},{7,5},{8,14},{9,15},{10,... | collective-permute-start | bytes 1179656 | tf_op jit(solution)/shard_map/ppermute | solution.py:445
  52.9 28.0 %copy-start.1 = (s32[4,256]{1,0:T(4,128)S(1)}, s32[4,256]{1,0:T(4,128)}, u32[]{:S(2)}) copy-start(s32[4,256]{1,0:T(4,128)} %onset.1) | copy-start | bytes 12292
  106.7 13.1 %collective-permute-start.10 = (bf16[12,16,1024]{2,1,0:T(8,128)(2,1)S(1)}, bf16[12,16,1024]{2,1,0:T(8,128)(2,1)S(1)}, u32[]{:S(2)}, u32[]{:S(2)}) collective-permute-start(bf16[12,16,1024]{2,1,0:T(8,128)(2,1)S(1)} %get-tuple-element.35), channel_id=1, source_target_pairs={{0,2},{1,3},{2,4},{3,5},{4,6},{5,7},{6,0},{7,1},{8,10},{9,11},{10,... | collective-permute-start | bytes 1179656 | tf_op jit(solution)/shard_map/ppermute | solution.py:445
  107.9 16.1 %collective-permute-start.7 = (bf16[12,16,1024]{2,1,0:T(8,128)(2,1)S(1)}, bf16[12,16,1024]{2,1,0:T(8,128)(2,1)S(1)}, u32[]{:S(2)}, u32[]{:S(2)}) collective-permute-start(bf16[12,16,1024]{2,1,0:T(8,128)(2,1)S(1)} %get-tuple-element.31), channel_id=1, source_target_pairs={{0,6},{1,7},{2,0},{3,1},{4,2},{5,3},{6,4},{7,5},{8,14},{9,15},{10,... | collective-permute-start | bytes 1179656 | tf_op jit(solution)/shard_map/ppermute | solution.py:445
  110.6 17.9 %collective-permute-start.12 = (bf16[12,16,1024]{2,1,0:T(8,128)(2,1)S(1)}, bf16[12,16,1024]{2,1,0:T(8,128)(2,1)S(1)}, u32[]{:S(2)}, u32[]{:S(2)}) collective-permute-start(bf16[12,16,1024]{2,1,0:T(8,128)(2,1)S(1)} %get-tuple-element.36), channel_id=1, source_target_pairs={{0,6},{1,7},{2,0},{3,1},{4,2},{5,3},{6,4},{7,5},{8,14},{9,15},{10,... | collective-permute-start | bytes 1179656 | tf_op jit(solution)/shard_map/ppermute | solution.py:445
  120.0 13.4 %collective-permute-start.11 = (bf16[12,16,1024]{2,1,0:T(8,128)(2,1)S(1)}, bf16[12,16,1024]{2,1,0:T(8,128)(2,1)S(1)}, u32[]{:S(2)}, u32[]{:S(2)}) collective-permute-start(bf16[12,16,1024]{2,1,0:T(8,128)(2,1)S(1)} %add_convert_fusion.1), channel_id=1, source_target_pairs={{0,2},{1,3},{2,4},{3,5},{4,6},{5,7},{6,0},{7,1},{8,10},{9,11},{10,... | collective-permute-start | bytes 1179656 | tf_op jit(solution)/shard_map/ppermute | solution.py:445
  123.3 25.8 %copy-start.2 = (s32[8,64]{1,0:T(8,128)S(1)}, s32[8,64]{1,0:T(8,128)}, u32[]{:S(2)}) copy-start(s32[8,64]{1,0:T(8,128)} %param.9) | copy-start | bytes 6148
  123.3 34.9 %copy-start = (bf16[8,64,2048]{2,1,0:T(8,128)(2,1)S(1)}, bf16[8,64,2048]{2,1,0:T(8,128)(2,1)}, u32[]{:S(2)}) copy-start(bf16[8,64,2048]{2,1,0:T(8,128)(2,1)} %param.6) | copy-start | bytes 6291460
  123.3 17.1 %collective-permute-start.9 = (bf16[12,16,1024]{2,1,0:T(8,128)(2,1)S(1)}, bf16[12,16,1024]{2,1,0:T(8,128)(2,1)S(1)}, u32[]{:S(2)}, u32[]{:S(2)}) collective-permute-start(bf16[12,16,1024]{2,1,0:T(8,128)(2,1)S(1)} %get-tuple-element.32), channel_id=1, source_target_pairs={{0,2},{1,3},{2,4},{3,5},{4,6},{5,7},{6,0},{7,1},{8,10},{9,11},{10,... | collective-permute-start | bytes 1179656 | tf_op jit(solution)/shard_map/ppermute | solution.py:445
  124.1 16.3 %collective-permute-start.8 = (bf16[12,16,1024]{2,1,0:T(8,128)(2,1)S(1)}, bf16[12,16,1024]{2,1,0:T(8,128)(2,1)S(1)}, u32[]{:S(2)}, u32[]{:S(2)}) collective-permute-start(bf16[12,16,1024]{2,1,0:T(8,128)(2,1)S(1)} %add_convert_fusion.2), channel_id=1, source_target_pairs={{0,6},{1,7},{2,0},{3,1},{4,2},{5,3},{6,4},{7,5},{8,14},{9,15},{10,... | collective-permute-start | bytes 1179656 | tf_op jit(solution)/shard_map/ppermute | solution.py:445
  133.7 9.8 %collective-permute-start.13 = (bf16[12,16,1024]{2,1,0:T(8,128)(2,1)S(1)}, bf16[12,16,1024]{2,1,0:T(8,128)(2,1)S(1)}, u32[]{:S(2)}, u32[]{:S(2)}) collective-permute-start(bf16[12,16,1024]{2,1,0:T(8,128)(2,1)S(1)} %add_convert_fusion), channel_id=1, source_target_pairs={{0,1},{1,0},{2,3},{3,2},{4,5},{5,4},{6,7},{7,6},{8,9},{9,8},{10,11... | collective-permute-start | bytes 1179656 | tf_op jit(solution)/shard_map/ppermute | solution.py:445
  145.3 12.8 %all-to-all-start.3 = ((bf16[16,12,8,128]{3,2,1,0:T(8,128)(2,1)}), bf16[16,12,8,128]{3,2,1,0:T(8,128)(2,1)S(1)}, u32[]{:S(2)}, u32[]{:S(2)}) async-start(bf16[16,12,8,128]{3,2,1,0:T(8,128)(2,1)} %fold.1), calls=%async_computation.3 | async-start | bytes 786432 | tf_op jit(solution)/shard_map/all_to_all | solution.py:453

commit v3 on v2

--- a/solution.py
+++ b/solution.py
@@ -173,9 +173,15 @@
     return [2 * ((y + dy) % NY) + (z + dz) % 2 for dy, dz in RELATIVE]
 
 
-def hold_body(kern, held, sems):
+KEPT = 2
+
+
+def hold_body(kern, held, kept, sems):
     copies = [
         pltpu.make_async_copy(kern.at[part], held.at[part], sems.at[part]) for part in range(2)
+    ] + [
+        pltpu.make_async_copy(kern.at[part, :KEPT], kept.at[part], sems.at[2 + part])
+        for part in range(2)
     ]
     for copy in copies:
         copy.start()
@@ -187,9 +193,12 @@
     return pl.pallas_call(
         hold_body,
         in_specs=[HBM_SPEC],
-        out_specs=pl.BlockSpec(memory_space=pl.ANY),
-        out_shape=pltpu.VMEM(kern.shape, BF16),
-        scratch_shapes=[pltpu.SemaphoreType.DMA((2,))],
+        out_specs=[pl.BlockSpec(memory_space=pl.ANY)] * 2,
+        out_shape=[
+            pltpu.VMEM(kern.shape, BF16),
+            pltpu.VMEM((2, KEPT) + kern.shape[2:], BF16),
+        ],
+        scratch_shapes=[pltpu.SemaphoreType.DMA((4,))],
         compiler_params=pltpu.CompilerParams(vmem_limit_bytes=1 << 20),
         cost_estimate=cost(0, 13 << 20),
         name="hold",
@@ -241,7 +250,7 @@
         outs[index][j] = terms[index * 16 : index * 16 + 16]
 
 
-def adjoint_remote_body(me, field_ref, kern, *refs):
+def adjoint_remote_body(me, field_ref, kern, kept, *refs):
     *outs, held, sems = refs
     place = places(me[0])
 
@@ -252,8 +261,11 @@
         ]
 
     for at in range(J):
-        for copy in copies(at):
-            copy.start()
+        for part in range(2):
+            source = kept if at < KEPT else kern
+            pltpu.make_async_copy(
+                source.at[part, at], held.at[part, at], sems.at[part, at]
+            ).start()
 
     def step(j2, carry):
         for parity in range(BANDS):
@@ -265,18 +277,18 @@
     lax.fori_loop(0, J2, step, 0)
 
 
-def adjoint_remote(me, field, kern):
+def adjoint_remote(me, field, kern, kept):
     term = jax.ShapeDtypeStruct((J, 2 * POINTS, R), BF16)
     *terms, held = pl.pallas_call(
         adjoint_remote_body,
-        in_specs=[SMEM_SPEC, VMEM_SPEC, HBM_SPEC],
+        in_specs=[SMEM_SPEC, VMEM_SPEC, HBM_SPEC, VMEM_SPEC],
         out_specs=[VMEM_SPEC] * (len(REMOTE) + 1),
         out_shape=[term] * len(REMOTE) + [pltpu.VMEM(kern.shape, BF16)],
         scratch_shapes=[pltpu.SemaphoreType.DMA((2, J))],
         compiler_params=pltpu.CompilerParams(vmem_limit_bytes=8 << 20),
         cost_estimate=cost(4 * J * 64 * SOURCES * R, 14 << 20),
         name="adjoint_remote",
-    )(me, field, kern)
+    )(me, field, kern, kept)
     return terms, held
 
 
@@ -409,7 +421,8 @@
     for p in range(UP_POINTS):
         every = pl.ds(p, ROWS, stride=UP_POINTS)
         bands = [wide.at[parity][every, :].astype(BF16) for parity in range(BANDS)]
-        limit = onset[:, p].reshape(2 * RECV, 1)
+        row = jnp.concatenate([onset[p : p + 1, :], onset[p + 4 : p + 5, :]], axis=1).astype(F32)
+        limit = jnp.broadcast_to(row, (128, 2 * RECV)).T[:, :1].astype(jnp.int32)
         for half, trace in enumerate(inverse_bands(table, bands)):
             span = slice(half * HT, half * HT + HT)
             cut = jnp.where(sample < limit - half * HT, trace, 0.0)
@@ -455,19 +468,18 @@
 
 def whole(focusing, direct, kernel, onset_up, onset_back):
     me = lax.axis_index("src").reshape(1)
-    back_onset = onset_back.reshape(2, UP_POINTS, RECV, 1)
     kernel = pltpu.with_memory_space_constraint(kernel, pltpu.HBM)
 
     traces = focusing.reshape(2, UP_POINTS, RECV, NT)
     table, bins = spectrum(pltpu.with_memory_space_constraint(traces, pltpu.HBM))
-    bins, me, back_onset = lax.optimization_barrier((bins, me, back_onset))
+    bins, me = lax.optimization_barrier((bins, me))
     own = unfold(exchange(bins).reshape(NFREQ, J, 8, 128))
     own, late_kernel = lax.optimization_barrier((own, kernel))
 
     across = shift(own, 0, 1)
     up = shift(own, 1, 0)
     down = shift(own, -1, 0)
-    held = hold(pltpu.with_memory_space_constraint(late_kernel, pltpu.HBM))
+    held, kept = hold(pltpu.with_memory_space_constraint(late_kernel, pltpu.HBM))
     across_down = shift(across, -1, 0)
     across_up = shift(across, 1, 0)
     far = shift(up, 1, 0)
@@ -478,7 +490,7 @@
     upgoing, back = truncate(waves.reshape(NFREQ * J * 8, SOURCES), table, onset_up)
     back = exchange(back.reshape(NFREQ, J, 8, SOURCES))
 
-    (far, across_up, across_down, across_far), held = adjoint_remote(me, back, kernel)
+    (far, across_up, across_down, across_far), held = adjoint_remote(me, back, kernel, kept)
     own, up, down, across = adjoint_near(me, back, held)
     r1 = shift(across_far, 1, 0)
     r5 = shift(far, -1, 0)
@@ -493,7 +505,7 @@
         summed.reshape(NFREQ * J * 8, 2 * RECV),
         table,
         direct.reshape(2, UP_POINTS, RECV, NT),
-        back_onset,
+        onset_back,
     )
     return (
         upgoing.reshape(UP_POINTS, SOURCES, NT),

time: 162 us -> 160 us (0.988)
  blocking collectives: 46.8 us -> 59.4 us
  waiting for transfers between devices: 51.4 us -> 41.9 us
  starting transfers between devices: 30.5 us -> 26.8 us
    all_to_all x3 -> x4, blocking collectives: 46.8 us -> 59.4 us  [exchange(): lax.all_to_all(value, 'freq', split_axis=0, concat_axis=0, tiled=True)]
    all_to_all x1 -> x0, waiting for transfers between devices: 8.91 us -> none  [exchange(): lax.all_to_all(value, 'freq', split_axis=0, concat_axis=0, tiled=True)]
    all_to_all x1 -> x0, starting transfers between devices: 3.73 us -> none  [exchange(): lax.all_to_all(value, 'freq', split_axis=0, concat_axis=0, tiled=True)]
  transfers between devices with their start and end apart: 15 -> 14, of which waited for: 11 -> 9; matrix products, arithmetic and copies ran while one was open for 0% -> 0% of each run, Pallas kernels for 5% -> 5%
where the time goes in v3:
time: 160 us; the launch traced here: 159 us
  blocking collectives  59.4 us (37%)
  waiting for transfers between devices  41.9 us (26%)
  Pallas kernels  29.9 us (19%)
  starting transfers between devices  26.8 us (17%)
    all_to_all x4, blocking collectives, exchange(): lax.all_to_all(value, 'freq', split_axis=0, concat_axis=0, tiled=True)  59.4 us
    ppermute x14, waiting for transfers between devices, shift(): return lax.ppermute(value, 'src', pairs)  41.9 us
    ppermute x14, starting transfers between devices, shift(): return lax.ppermute(value, 'src', pairs)  26.8 us
    pallas_call x1, Pallas kernels, hold(): pl.pallas_call(hold_body, in_specs=[HBM_SPEC], out_specs=[pl.BlockSpec(me...  5.16 us
    pallas_call x1, Pallas kernels, forward(): pl.pallas_call(forward_body, in_specs=[SMEM_SPEC] + [VMEM_SPEC] * (NSRC +...  4.89 us
    pallas_call x1, Pallas kernels, truncate(): pl.pallas_call(truncate_body, in_specs=[VMEM_SPEC] * 3, out_specs=[pl.Blo...  4.83 us
    pallas_call x1, Pallas kernels, adjoint_remote(): pl.pallas_call(adjoint_remote_body, in_specs=[SMEM_SPEC, VMEM_SPEC, HBM_S...  4.65 us
  transfers between devices with their start and end apart: 14, of which 9 were waited for; matrix products, arithmetic and copies ran while one was open for 0% of the time, Pallas kernels for 5%

profile of v3, /device:TPU:0, one launch (start us, length us, event | category | flops | bytes accessed | tf_op | source)
XLA Modules:
  0.0 159.3 jit_solution(14537345831893007202)
XLA Ops:
  0.6 2.9 %spectrum.1 = (bf16[2,192,1024]{2,1,0:T(8,128)(2,1)S(1)}, bf16[16,2,48,128]{3,2,1,0:T(8,128)(2,1)S(1)}) custom-call(bf16[2,4,64,2048]{3,2,1,0:T(8,128)(2,1)} %bitcast.14), custom_call_target="tpu_custom_call" | custom-call | flops 402653184 | bytes 4194304 | tf_op jit(solution)/shard_map/spectrum/pallas_call | solution.py:118
  3.5 14.7 %all_to_all.20 = bf16[16,2,48,128]{3,2,1,0:T(8,128)(2,1)S(1)} all-to-all(bf16[16,2,48,128]{3,2,1,0:T(8,128)(2,1)S(1)} %get-tuple-element.23), channel_id=1, replica_groups=mesh['freq'=16,'src'=8] {'freq'}, dimensions={0} | all-to-all | bytes 786432 | tf_op jit(solution)/shard_map/all_to_all | solution.py:466
  18.2 1.0 unfold.1.refs_0_
  19.2 3.7 %collective-permute-start.3 = (bf16[12,16,1024]{2,1,0:T(8,128)(2,1)S(1)}, bf16[12,16,1024]{2,1,0:T(8,128)(2,1)S(1)}, u32[]{:S(2)}, u32[]{:S(2)}) collective-permute-start(bf16[12,16,1024]{2,1,0:T(8,128)(2,1)S(1)} %unfold.1.refs_0_), channel_id=1, source_target_pairs={{0,1},{1,0},{2,3},{3,2},{4,5},{5,4},{6,7},{7,6},{8,9},{9,8},{10,11... | collective-permute-start | bytes 1179656 | tf_op jit(solution)/shard_map/ppermute | solution.py:458
  22.9 1.6 collective-permute-start
  24.5 7.6 %collective-permute-done.3.refs_4_ = bf16[12,16,1024]{2,1,0:T(8,128)(2,1)S(1)} collective-permute-done((bf16[12,16,1024]{2,1,0:T(8,128)(2,1)S(1)}, bf16[12,16,1024]{2,1,0:T(8,128)(2,1)S(1)}, u32[]{:S(2)}, u32[]{:S(2)}) %collective-permute-start.3) | collective-permute-done | bytes 393248 | tf_op jit(solution)/shard_map/ppermute | solution.py:458
  32.1 3.0 %collective-permute-start.5 = (bf16[12,16,1024]{2,1,0:T(8,128)(2,1)S(1)}, bf16[12,16,1024]{2,1,0:T(8,128)(2,1)S(1)}, u32[]{:S(2)}, u32[]{:S(2)}) collective-permute-start(bf16[12,16,1024]{2,1,0:T(8,128)(2,1)S(1)} %collective-permute-done.3.refs_4_), channel_id=1, source_target_pairs={{0,6},{1,7},{2,0},{3,1},{4,2},{5,3},{6,4},{7,5},{8,14},{9,15},{10,... | collective-permute-start | bytes 1179656 | tf_op jit(solution)/shard_map/ppermute | solution.py:458
  35.9 1.3 collective-permute-start.4
  37.2 7.5 %collective-permute-done.5.refs_6_ = bf16[12,16,1024]{2,1,0:T(8,128)(2,1)S(1)} collective-permute-done((bf16[12,16,1024]{2,1,0:T(8,128)(2,1)S(1)}, bf16[12,16,1024]{2,1,0:T(8,128)(2,1)S(1)}, u32[]{:S(2)}, u32[]{:S(2)}) %collective-permute-start.5) | collective-permute-done | bytes 393248 | tf_op jit(solution)/shard_map/ppermute | solution.py:458
  44.6 3.7 %collective-permute-start.6 = (bf16[12,16,1024]{2,1,0:T(8,128)(2,1)S(1)}, bf16[12,16,1024]{2,1,0:T(8,128)(2,1)S(1)}, u32[]{:S(2)}, u32[]{:S(2)}) collective-permute-start(bf16[12,16,1024]{2,1,0:T(8,128)(2,1)S(1)} %collective-permute-done.5.refs_6_), channel_id=1, source_target_pairs={{0,6},{1,7},{2,0},{3,1},{4,2},{5,3},{6,4},{7,5},{8,14},{9,15},{10,... | collective-permute-start | bytes 1179656 | tf_op jit(solution)/shard_map/ppermute | solution.py:458
  48.3 5.2 %hold.1 = (bf16[2,12,256,1024]{3,2,1,0:T(8,128)(2,1)S(1)}, bf16[2,2,256,1024]{3,2,1,0:T(8,128)(2,1)S(1)}) custom-call(bf16[2,12,256,1024]{3,2,1,0:T(8,128)(2,1)} %kern.2), custom_call_target="tpu_custom_call" | custom-call | bytes 13631488 | tf_op jit(solution)/shard_map/hold/pallas_call | solution.py:193
  53.5 1.8 %collective-permute-done.2.refs_3_ = bf16[12,16,1024]{2,1,0:T(8,128)(2,1)S(1)} collective-permute-done((bf16[12,16,1024]{2,1,0:T(8,128)(2,1)S(1)}, bf16[12,16,1024]{2,1,0:T(8,128)(2,1)S(1)}, u32[]{:S(2)}, u32[]{:S(2)}) %collective-permute-start.2) | collective-permute-done | bytes 393248 | tf_op jit(solution)/shard_map/ppermute | solution.py:458
  55.3 4.6 %collective-permute-done.6.refs_7_ = bf16[12,16,1024]{2,1,0:T(8,128)(2,1)S(1)} collective-permute-done((bf16[12,16,1024]{2,1,0:T(8,128)(2,1)S(1)}, bf16[12,16,1024]{2,1,0:T(8,128)(2,1)S(1)}, u32[]{:S(2)}, u32[]{:S(2)}) %collective-permute-start.6) | collective-permute-done | bytes 393248 | tf_op jit(solution)/shard_map/ppermute | solution.py:458
  59.9 4.9 %forward.1 = bf16[16,12,8,256]{3,2,1,0:T(8,128)(2,1)S(1)} custom-call(s32[1]{0:T(128)} %bitcast.1.me, bf16[12,16,1024]{2,1,0:T(8,128)(2,1)S(1)} %unfold.1.refs_0_, bf16[12,16,1024]{2,1,0:T(8,128)(2,1)S(1)} %collective-permute-done.refs_1_, bf16[12,16,1024]{2,1,0:T(8,128)(2,1)S(1)} %collective-permute-done.1.refs_2_, ...), custom_call_target="tpu_custom_call" | custom-call | flops 1610612736 | bytes 4194304 | tf_op jit(solution)/shard_map/forward/pallas_call | solution.py:229
  64.8 16.1 %all_to_all.21 = bf16[16,12,8,256]{3,2,1,0:T(8,128)(2,1)S(1)} all-to-all(bf16[16,12,8,256]{3,2,1,0:T(8,128)(2,1)S(1)} %forward.1), channel_id=1, replica_groups=mesh['freq'=16,'src'=8] {'freq'}, dimensions={0} | all-to-all | bytes 1572864 | tf_op jit(solution)/shard_map/all_to_all | solution.py:466
  80.9 4.8 %truncate.1 = (bf16[1024,2048]{1,0:T(8,128)(2,1)}, bf16[1536,256]{1,0:T(8,128)(2,1)S(1)}) custom-call(bf16[1536,256]{1,0:T(8,128)(2,1)S(1)} %bitcast.12, bf16[2,192,1024]{2,1,0:T(8,128)(2,1)S(1)} %get-tuple-element.27.table, s32[4,256]{1,0:T(4,128)S(1)} %copy-done.2), custom_call_target="tpu_custom_call" | custom-call | flops 1610612736 | bytes 8388608 | tf_op jit(solution)/shard_map/truncate/pallas_call | solution.py:397
  85.7 15.9 %all_to_all.22.field_ref = bf16[16,12,8,256]{3,2,1,0:T(8,128)(2,1)S(1)} all-to-all(bf16[16,12,8,256]{3,2,1,0:T(8,128)(2,1)S(1)} %bitcast.13), channel_id=1, replica_groups=mesh['freq'=16,'src'=8] {'freq'}, dimensions={0} | all-to-all | bytes 1572864 | tf_op jit(solution)/shard_map/all_to_all | solution.py:466
  101.6 4.6 %adjoint_remote.1 = (bf16[12,16,1024]{2,1,0:T(8,128)(2,1)S(1)}, bf16[12,16,1024]{2,1,0:T(8,128)(2,1)S(1)}, bf16[12,16,1024]{2,1,0:T(8,128)(2,1)S(1)}, bf16[12,16...) custom-call(s32[1]{0:T(128)} %bitcast.1.me, bf16[16,12,8,256]{3,2,1,0:T(8,128)(2,1)S(1)} %all_to_all.22.field_ref, ...), custom_call_target="tpu_custom_call" | custom-call | flops 805306368 | bytes 14680064 | tf_op jit(solution)/shard_map/adjoint_remote/pallas_call | solution.py:282
  106.3 1.1 collective-permute-start.10
  107.4 2.7 %collective-permute-start.7 = (bf16[12,16,1024]{2,1,0:T(8,128)(2,1)S(1)}, bf16[12,16,1024]{2,1,0:T(8,128)(2,1)S(1)}, u32[]{:S(2)}, u32[]{:S(2)}) collective-permute-start(bf16[12,16,1024]{2,1,0:T(8,128)(2,1)S(1)} %get-tuple-element.34), channel_id=1, source_target_pairs={{0,6},{1,7},{2,0},{3,1},{4,2},{5,3},{6,4},{7,5},{8,14},{9,15},{10,... | collective-permute-start | bytes 1179656 | tf_op jit(solution)/shard_map/ppermute | solution.py:458
  110.1 1.9 %collective-permute-start.12 = (bf16[12,16,1024]{2,1,0:T(8,128)(2,1)S(1)}, bf16[12,16,1024]{2,1,0:T(8,128)(2,1)S(1)}, u32[]{:S(2)}, u32[]{:S(2)}) collective-permute-start(bf16[12,16,1024]{2,1,0:T(8,128)(2,1)S(1)} %get-tuple-element.39), channel_id=1, source_target_pairs={{0,6},{1,7},{2,0},{3,1},{4,2},{5,3},{6,4},{7,5},{8,14},{9,15},{10,... | collective-permute-start | bytes 1179656 | tf_op jit(solution)/shard_map/ppermute | solution.py:458
  112.1 7.3 %collective-permute-done.10 = bf16[12,16,1024]{2,1,0:T(8,128)(2,1)S(1)} collective-permute-done((bf16[12,16,1024]{2,1,0:T(8,128)(2,1)S(1)}, bf16[12,16,1024]{2,1,0:T(8,128)(2,1)S(1)}, u32[]{:S(2)}, u32[]{:S(2)}) %collective-permute-start.10) | collective-permute-done | bytes 393248 | tf_op jit(solution)/shard_map/ppermute | solution.py:458
  119.8 3.0 %adjoint_near.1 = (bf16[12,16,1024]{2,1,0:T(8,128)(2,1)S(1)}, bf16[12,16,1024]{2,1,0:T(8,128)(2,1)S(1)}, bf16[12,16,1024]{2,1,0:T(8,128)(2,1)S(1)}, bf16[12,16,1024]{2,1,0:T(8,128)(2,1)S(1)}) custom-call(s32[1]{0:T(128)} %bitcast.1.me, bf16[16,12,8,256]{3,2,1,0:T(8,128)(2,1)S(1)} %all_to_all.22.field_ref, bf16[2,12,256,1024]{3,2,1,0:T(8,128)(2,1)S(1)} %get-tuple-element.31.held), custom_call_target="tpu_custom_call" | custom-call | flops 805306368 | bytes 2097152 | tf_op jit(solution)/shard_map/adjoint_near/pallas_call | solution.py:307
  123.7 2.7 %collective-permute-start.8 = (bf16[12,16,1024]{2,1,0:T(8,128)(2,1)S(1)}, bf16[12,16,1024]{2,1,0:T(8,128)(2,1)S(1)}, u32[]{:S(2)}, u32[]{:S(2)}) collective-permute-start(bf16[12,16,1024]{2,1,0:T(8,128)(2,1)S(1)} %add_convert_fusion.2), channel_id=1, source_target_pairs={{0,6},{1,7},{2,0},{3,1},{4,2},{5,3},{6,4},{7,5},{8,14},{9,15},{10,... | collective-permute-start | bytes 1179656 | tf_op jit(solution)/shard_map/ppermute | solution.py:458
  126.3 1.7 %collective-permute-done.12 = bf16[12,16,1024]{2,1,0:T(8,128)(2,1)S(1)} collective-permute-done((bf16[12,16,1024]{2,1,0:T(8,128)(2,1)S(1)}, bf16[12,16,1024]{2,1,0:T(8,128)(2,1)S(1)}, u32[]{:S(2)}, u32[]{:S(2)}) %collective-permute-start.12) | collective-permute-done | bytes 393248 | tf_op jit(solution)/shard_map/ppermute | solution.py:458
  128.0 4.9 %collective-permute-done.11 = bf16[12,16,1024]{2,1,0:T(8,128)(2,1)S(1)} collective-permute-done((bf16[12,16,1024]{2,1,0:T(8,128)(2,1)S(1)}, bf16[12,16,1024]{2,1,0:T(8,128)(2,1)S(1)}, u32[]{:S(2)}, u32[]{:S(2)}) %collective-permute-start.11) | collective-permute-done | bytes 393248 | tf_op jit(solution)/shard_map/ppermute | solution.py:458
  133.2 3.4 %collective-permute-start.13 = (bf16[12,16,1024]{2,1,0:T(8,128)(2,1)S(1)}, bf16[12,16,1024]{2,1,0:T(8,128)(2,1)S(1)}, u32[]{:S(2)}, u32[]{:S(2)}) collective-permute-start(bf16[12,16,1024]{2,1,0:T(8,128)(2,1)S(1)} %add_convert_fusion), channel_id=1, source_target_pairs={{0,1},{1,0},{2,3},{3,2},{4,5},{5,4},{6,7},{7,6},{8,9},{9,8},{10,11... | collective-permute-start | bytes 1179656 | tf_op jit(solution)/shard_map/ppermute | solution.py:458
  136.5 3.4 %collective-permute-done.9.refs_2_ = bf16[12,16,1024]{2,1,0:T(8,128)(2,1)S(1)} collective-permute-done((bf16[12,16,1024]{2,1,0:T(8,128)(2,1)S(1)}, bf16[12,16,1024]{2,1,0:T(8,128)(2,1)S(1)}, u32[]{:S(2)}, u32[]{:S(2)}) %collective-permute-start.9) | collective-permute-done | bytes 393248 | tf_op jit(solution)/shard_map/ppermute | solution.py:458
  140.0 3.1 %collective-permute-done.13.refs_3_ = bf16[12,16,1024]{2,1,0:T(8,128)(2,1)S(1)} collective-permute-done((bf16[12,16,1024]{2,1,0:T(8,128)(2,1)S(1)}, bf16[12,16,1024]{2,1,0:T(8,128)(2,1)S(1)}, u32[]{:S(2)}, u32[]{:S(2)}) %collective-permute-start.13) | collective-permute-done | bytes 393248 | tf_op jit(solution)/shard_map/ppermute | solution.py:458
  143.0 1.1 fold.1
  144.1 12.6 %all_to_all.23 = bf16[16,12,8,128]{3,2,1,0:T(8,128)(2,1)S(1)} all-to-all(bf16[16,12,8,128]{3,2,1,0:T(8,128)(2,1)S(1)} %fold.1), channel_id=1, replica_groups=mesh['freq'=16,'src'=8] {'freq'}, dimensions={0} | all-to-all | bytes 786432 | tf_op jit(solution)/shard_map/all_to_all | solution.py:466
  156.7 2.5 %update.1 = bf16[2,4,64,2048]{3,2,1,0:T(8,128)(2,1)} custom-call(bf16[1536,128]{1,0:T(8,128)(2,1)S(1)} %bitcast.10, bf16[2,192,1024]{2,1,0:T(8,128)(2,1)S(1)} %get-tuple-element.27.table, bf16[2,4,64,2048]{3,2,1,0:T(8,128)(2,1)S(1)} %bitcast.9, s32[8,64]{1,0:T(8,128)S(1)} %copy-done.1), custom_call_target="tpu_custom_call" | custom-call | flops 402653184 | bytes 5242880 | tf_op jit(solution)/shard_map/update/pallas_call | solution.py:438
  (18 shorter events, 2.2 us)
Async XLA Ops:
  19.2 12.9 %collective-permute-start.3 = (bf16[12,16,1024]{2,1,0:T(8,128)(2,1)S(1)}, bf16[12,16,1024]{2,1,0:T(8,128)(2,1)S(1)}, u32[]{:S(2)}, u32[]{:S(2)}) collective-permute-start(bf16[12,16,1024]{2,1,0:T(8,128)(2,1)S(1)} %unfold.1.refs_0_), channel_id=1, source_target_pairs={{0,1},{1,0},{2,3},{3,2},{4,5},{5,4},{6,7},{7,6},{8,9},{9,8},{10,11... | collective-permute-start | bytes 1179656 | tf_op jit(solution)/shard_map/ppermute | solution.py:458
  22.9 14.3 %collective-permute-start = (bf16[12,16,1024]{2,1,0:T(8,128)(2,1)S(1)}, bf16[12,16,1024]{2,1,0:T(8,128)(2,1)S(1)}, u32[]{:S(2)}, u32[]{:S(2)}) collective-permute-start(bf16[12,16,1024]{2,1,0:T(8,128)(2,1)S(1)} %unfold.1.refs_0_), channel_id=1, source_target_pairs={{0,2},{1,3},{2,4},{3,5},{4,6},{5,7},{6,0},{7,1},{8,10},{9,11},{10,... | collective-permute-start | bytes 1179656 | tf_op jit(solution)/shard_map/ppermute | solution.py:458
  32.1 12.5 %collective-permute-start.5 = (bf16[12,16,1024]{2,1,0:T(8,128)(2,1)S(1)}, bf16[12,16,1024]{2,1,0:T(8,128)(2,1)S(1)}, u32[]{:S(2)}, u32[]{:S(2)}) collective-permute-start(bf16[12,16,1024]{2,1,0:T(8,128)(2,1)S(1)} %collective-permute-done.3.refs_4_), channel_id=1, source_target_pairs={{0,6},{1,7},{2,0},{3,1},{4,2},{5,3},{6,4},{7,5},{8,14},{9,15},{10,... | collective-permute-start | bytes 1179656 | tf_op jit(solution)/shard_map/ppermute | solution.py:458
  35.1 18.4 %collective-permute-start.1 = (bf16[12,16,1024]{2,1,0:T(8,128)(2,1)S(1)}, bf16[12,16,1024]{2,1,0:T(8,128)(2,1)S(1)}, u32[]{:S(2)}, u32[]{:S(2)}) collective-permute-start(bf16[12,16,1024]{2,1,0:T(8,128)(2,1)S(1)} %unfold.1.refs_0_), channel_id=1, source_target_pairs={{0,6},{1,7},{2,0},{3,1},{4,2},{5,3},{6,4},{7,5},{8,14},{9,15},{10,... | collective-permute-start | bytes 1179656 | tf_op jit(solution)/shard_map/ppermute | solution.py:458
  35.9 17.6 %collective-permute-start.4 = (bf16[12,16,1024]{2,1,0:T(8,128)(2,1)S(1)}, bf16[12,16,1024]{2,1,0:T(8,128)(2,1)S(1)}, u32[]{:S(2)}, u32[]{:S(2)}) collective-permute-start(bf16[12,16,1024]{2,1,0:T(8,128)(2,1)S(1)} %collective-permute-done.3.refs_4_), channel_id=1, source_target_pairs={{0,2},{1,3},{2,4},{3,5},{4,6},{5,7},{6,0},{7,1},{8,10},{9,11},{10,... | collective-permute-start | bytes 1179656 | tf_op jit(solution)/shard_map/ppermute | solution.py:458
  37.1 18.2 %collective-permute-start.2 = (bf16[12,16,1024]{2,1,0:T(8,128)(2,1)S(1)}, bf16[12,16,1024]{2,1,0:T(8,128)(2,1)S(1)}, u32[]{:S(2)}, u32[]{:S(2)}) collective-permute-start(bf16[12,16,1024]{2,1,0:T(8,128)(2,1)S(1)} %collective-permute-done.refs_1_), channel_id=1, source_target_pairs={{0,2},{1,3},{2,4},{3,5},{4,6},{5,7},{6,0},{7,1},{8,10},{9,11},{10,... | collective-permute-start | bytes 1179656 | tf_op jit(solution)/shard_map/ppermute | solution.py:458
  44.6 15.2 %collective-permute-start.6 = (bf16[12,16,1024]{2,1,0:T(8,128)(2,1)S(1)}, bf16[12,16,1024]{2,1,0:T(8,128)(2,1)S(1)}, u32[]{:S(2)}, u32[]{:S(2)}) collective-permute-start(bf16[12,16,1024]{2,1,0:T(8,128)(2,1)S(1)} %collective-permute-done.5.refs_6_), channel_id=1, source_target_pairs={{0,6},{1,7},{2,0},{3,1},{4,2},{5,3},{6,4},{7,5},{8,14},{9,15},{10,... | collective-permute-start | bytes 1179656 | tf_op jit(solution)/shard_map/ppermute | solution.py:458
  59.9 21.0 %copy-start.2 = (s32[4,256]{1,0:T(4,128)S(1)}, s32[4,256]{1,0:T(4,128)}, u32[]{:S(2)}) copy-start(s32[4,256]{1,0:T(4,128)} %onset.2) | copy-start | bytes 12292
  106.3 13.1 %collective-permute-start.10 = (bf16[12,16,1024]{2,1,0:T(8,128)(2,1)S(1)}, bf16[12,16,1024]{2,1,0:T(8,128)(2,1)S(1)}, u32[]{:S(2)}, u32[]{:S(2)}) collective-permute-start(bf16[12,16,1024]{2,1,0:T(8,128)(2,1)S(1)} %get-tuple-element.38), channel_id=1, source_target_pairs={{0,2},{1,3},{2,4},{3,5},{4,6},{5,7},{6,0},{7,1},{8,10},{9,11},{10,... | collective-permute-start | bytes 1179656 | tf_op jit(solution)/shard_map/ppermute | solution.py:458
  107.4 16.1 %collective-permute-start.7 = (bf16[12,16,1024]{2,1,0:T(8,128)(2,1)S(1)}, bf16[12,16,1024]{2,1,0:T(8,128)(2,1)S(1)}, u32[]{:S(2)}, u32[]{:S(2)}) collective-permute-start(bf16[12,16,1024]{2,1,0:T(8,128)(2,1)S(1)} %get-tuple-element.34), channel_id=1, source_target_pairs={{0,6},{1,7},{2,0},{3,1},{4,2},{5,3},{6,4},{7,5},{8,14},{9,15},{10,... | collective-permute-start | bytes 1179656 | tf_op jit(solution)/shard_map/ppermute | solution.py:458
  110.1 17.9 %collective-permute-start.12 = (bf16[12,16,1024]{2,1,0:T(8,128)(2,1)S(1)}, bf16[12,16,1024]{2,1,0:T(8,128)(2,1)S(1)}, u32[]{:S(2)}, u32[]{:S(2)}) collective-permute-start(bf16[12,16,1024]{2,1,0:T(8,128)(2,1)S(1)} %get-tuple-element.39), channel_id=1, source_target_pairs={{0,6},{1,7},{2,0},{3,1},{4,2},{5,3},{6,4},{7,5},{8,14},{9,15},{10,... | collective-permute-start | bytes 1179656 | tf_op jit(solution)/shard_map/ppermute | solution.py:458
  119.5 13.4 %collective-permute-start.11 = (bf16[12,16,1024]{2,1,0:T(8,128)(2,1)S(1)}, bf16[12,16,1024]{2,1,0:T(8,128)(2,1)S(1)}, u32[]{:S(2)}, u32[]{:S(2)}) collective-permute-start(bf16[12,16,1024]{2,1,0:T(8,128)(2,1)S(1)} %add_convert_fusion.1), channel_id=1, source_target_pairs={{0,2},{1,3},{2,4},{3,5},{4,6},{5,7},{6,0},{7,1},{8,10},{9,11},{10,... | collective-permute-start | bytes 1179656 | tf_op jit(solution)/shard_map/ppermute | solution.py:458
  122.8 33.9 %copy-start = (bf16[8,64,2048]{2,1,0:T(8,128)(2,1)S(1)}, bf16[8,64,2048]{2,1,0:T(8,128)(2,1)}, u32[]{:S(2)}) copy-start(bf16[8,64,2048]{2,1,0:T(8,128)(2,1)} %param.6) | copy-start | bytes 6291460
  122.8 33.9 %copy-start.1 = (s32[8,64]{1,0:T(8,128)S(1)}, s32[8,64]{1,0:T(8,128)}, u32[]{:S(2)}) copy-start(s32[8,64]{1,0:T(8,128)} %onset.3) | copy-start | bytes 6148
  122.8 17.2 %collective-permute-start.9 = (bf16[12,16,1024]{2,1,0:T(8,128)(2,1)S(1)}, bf16[12,16,1024]{2,1,0:T(8,128)(2,1)S(1)}, u32[]{:S(2)}, u32[]{:S(2)}) collective-permute-start(bf16[12,16,1024]{2,1,0:T(8,128)(2,1)S(1)} %get-tuple-element.35), channel_id=1, source_target_pairs={{0,2},{1,3},{2,4},{3,5},{4,6},{5,7},{6,0},{7,1},{8,10},{9,11},{10,... | collective-permute-start | bytes 1179656 | tf_op jit(solution)/shard_map/ppermute | solution.py:458
  123.7 16.3 %collective-permute-start.8 = (bf16[12,16,1024]{2,1,0:T(8,128)(2,1)S(1)}, bf16[12,16,1024]{2,1,0:T(8,128)(2,1)S(1)}, u32[]{:S(2)}, u32[]{:S(2)}) collective-permute-start(bf16[12,16,1024]{2,1,0:T(8,128)(2,1)S(1)} %add_convert_fusion.2), channel_id=1, source_target_pairs={{0,6},{1,7},{2,0},{3,1},{4,2},{5,3},{6,4},{7,5},{8,14},{9,15},{10,... | collective-permute-start | bytes 1179656 | tf_op jit(solution)/shard_map/ppermute | solution.py:458
  133.2 9.8 %collective-permute-start.13 = (bf16[12,16,1024]{2,1,0:T(8,128)(2,1)S(1)}, bf16[12,16,1024]{2,1,0:T(8,128)(2,1)S(1)}, u32[]{:S(2)}, u32[]{:S(2)}) collective-permute-start(bf16[12,16,1024]{2,1,0:T(8,128)(2,1)S(1)} %add_convert_fusion), channel_id=1, source_target_pairs={{0,1},{1,0},{2,3},{3,2},{4,5},{5,4},{6,7},{7,6},{8,9},{9,8},{10,11... | collective-permute-start | bytes 1179656 | tf_op jit(solution)/shard_map/ppermute | solution.py:458
